TPU v7x, 256 devices: a whole 4x4x8 slice. The times are simulated.
256 devices in a mesh: mem: 16 (over z, y_lo), col: 16 (over y_hi, x, core).
Axes of the slice: x: 4, y: 4 (y_hi: 2, y_lo: 2; y = y_hi * 2 + y_lo), z: 8, core: 2. Of those that a mesh axis runs over, the one named last changes fastest.
Arguments:
- perturbations: bfloat16 [256, 262144], P('mem', 'col'), may hold values from -6 to 6
- obs_index: int32 [4, 256], replicated, may hold values from 0 to 262143, as said below
- obs_var: float32 [4, 256], replicated, may hold values from 1 to 8
Outputs:
- analysis: bfloat16 [256, 262144], P('mem', 'col')
Inputs may be any that keep to these rules, and one draw needn't show every extreme that they name: `obs_index`: within each batch, every aligned block of 1024 consecutive state indices holds exactly 1 of the batch's observations, all at different indices; their order within the batch is arbitrary.
All inputs are finite; a program needn't handle non-finite values.
Results may differ from a plain program's by a relative error of at most 0.0075.
Values may be sent and summed in bfloat16 or wider, within the bound.
No kernel may reach another device: no remote copies, remote signals or barrier semaphores. Data moves between devices by JAX's collectives and lax.ppermute only.
A program may use at most 64 MiB of HBM per device.

v0:
```python
import jax
import jax.numpy as jnp
from jax import lax
from jax.sharding import PartitionSpec as P


def transform_matrix(observed, variance, members):
    inverse_count = 1.0 / (members - 1)
    innov_cov = jnp.dot(
        observed.T, observed, preferred_element_type=jnp.float32
    ) * inverse_count + jnp.diag(variance)
    factor = jnp.linalg.cholesky(innov_cov)
    first_solve = jax.scipy.linalg.solve_triangular(
        factor, observed.T.astype(jnp.float32), lower=True
    )
    shifted = factor + jnp.diag(jnp.sqrt(variance))
    second = jax.scipy.linalg.solve_triangular(shifted, first_solve, trans=1, lower=True)
    product = jnp.dot(observed.astype(jnp.float32), second, precision=lax.Precision.HIGHEST)
    identity = jnp.eye(members, dtype=jnp.float32)
    return (identity - product * inverse_count).astype(jnp.bfloat16)


def observed_slots(indices, block_cols):
    blocks = indices // block_cols
    positions = jnp.arange(indices.shape[0], dtype=jnp.int32)
    same_block = blocks[:, None] == blocks[None, :]
    before = positions[None, :] < positions[:, None]
    rank_in_block = jnp.sum(jnp.where(same_block & before, 1, 0), axis=1).astype(jnp.int32)
    return (blocks, rank_in_block)


def pick_local(wanted, offsets):
    return jnp.sum(jnp.where(wanted, offsets[None, :], 0), axis=1)


def on_device(perturbations, obs_index, obs_var):
    members_here, group_cols = perturbations.shape
    mem_count = lax.axis_size("mem")
    col_count = lax.axis_size("col")
    members = members_here * mem_count
    block_cols = group_cols // mem_count
    batches, observations = obs_index.shape
    per_device = observations // (mem_count * col_count)
    mem_place = lax.axis_index("mem")
    col_place = lax.axis_index("col")
    my_block = col_place * mem_count + mem_place
    arranged = perturbations.reshape(members_here, mem_count, block_cols)
    ensemble = lax.all_to_all(arranged, "mem", split_axis=1, concat_axis=0, tiled=True).reshape(
        members, block_cols
    )
    for which_batch in range(batches):
        indices = obs_index[which_batch]
        blocks, rank_in_block = observed_slots(indices, block_cols)
        offsets = indices - blocks * block_cols
        wanted = (blocks == my_block)[None, :] & (
            rank_in_block[None, :] == jnp.arange(per_device, dtype=jnp.int32)[:, None]
        )
        owned_cols = jnp.take(ensemble, pick_local(wanted, offsets), axis=1)
        everyone = lax.all_gather(owned_cols, ("mem", "col"), axis=1, tiled=True)
        owners = blocks % mem_count * col_count + blocks // mem_count
        observed = jnp.take(everyone, owners * per_device + rank_in_block, axis=1)
        weights = transform_matrix(observed, obs_var[which_batch], members)
        ensemble = jnp.dot(weights, ensemble, preferred_element_type=jnp.float32).astype(
            jnp.bfloat16
        )
    returned = lax.all_to_all(
        ensemble.reshape(members, 1, block_cols), "mem", split_axis=0, concat_axis=1, tiled=True
    )
    return returned.reshape(members_here, group_cols)


def solution(mesh):
    return jax.shard_map(
        on_device,
        mesh=mesh,
        in_specs=(P("mem", "col"), P(), P()),
        out_specs=P("mem", "col"),
        check_vma=False,
    )
```

profile of v0, /device:TPU:2, one launch (start us, length us, event | category | flops | bytes accessed | tf_op | source)
XLA Modules:
  0.0 1777.1 jit_solution(7507499912998342137)
XLA Ops:
  0.0 1.9 copy.272
  1.9 9.7 all-to-all-start
  12.5 0.7 fusion.105
  20.8 0.7 copy-done.1
  21.6 7.2 all-to-all-done
  29.0 339.7 %all-gather = bf16[256,1,256]{2,1,0:T(2,128)(2,1)S(1)} all-gather(bf16[1,1,256]{2,1,0:T(2,128)(2,1)S(1)} %reshape.426), channel_id=1, replica_groups=mesh['mem'=16,'col'=16] {'mem','col'}, dimensions={0}, use_global_device_ids=true | all-gather | bytes 131584 | tf_op jit(solution)/shard_map/all_gather | solution.py:59
  368.6 1.2 gather_fusion
  370.3 11.7 cholesky.214
  382.0 9.8 custom-call.23
  392.3 12.2 cholesky.231
  405.0 0.6 compare_reduce_fusion.6
  407.6 4.1 while.17
  408.2 1.3 dynamic-slice.58
  410.3 1.3 dynamic-slice.58
  411.7 19.7 %custom-call.24 = f32[2,128,128]{1,2,0:T(8,128)S(1)} custom-call(f32[2,128,128]{2,1,0:T(8,128)S(1)} %get-tuple-element.73), custom_call_target="InvertDiagBlocksLowerTriangular" | custom-call | tf_op jit(solution)/shard_map/jit(_solve_triangular)/triangular_solve | solution.py:13
  432.4 4.2 while.18
  433.0 1.4 dynamic-slice.60
  435.1 1.4 dynamic-slice.60
  436.6 19.7 %custom-call.25 = f32[2,128,128]{1,2,0:T(8,128)S(1)} custom-call(f32[2,128,128]{2,1,0:T(8,128)S(1)} %get-tuple-element.74), custom_call_target="InvertDiagBlocksLowerTriangular" | custom-call | tf_op jit(solution)/shard_map/jit(_solve_triangular)/triangular_solve | solution.py:17
  458.1 342.6 %all-gather.1 = bf16[256,1,256]{2,1,0:T(2,128)(2,1)S(1)} all-gather(bf16[1,1,256]{2,1,0:T(2,128)(2,1)S(1)} %reshape.428), channel_id=1, replica_groups=mesh['mem'=16,'col'=16] {'mem','col'}, dimensions={0}, use_global_device_ids=true | all-gather | bytes 131584 | tf_op jit(solution)/shard_map/all_gather | solution.py:59
  800.7 1.2 gather_fusion.1
  802.3 11.7 cholesky.248
  814.1 9.8 custom-call.26
  824.4 11.9 cholesky.265
  836.7 0.7 compare_reduce_fusion.4
  837.4 0.6 compare_reduce_fusion.5
  839.5 4.2 while.19
  840.1 1.4 dynamic-slice.62
  842.2 1.4 dynamic-slice.62
  843.7 19.7 %custom-call.27 = f32[2,128,128]{1,2,0:T(8,128)S(1)} custom-call(f32[2,128,128]{2,1,0:T(8,128)S(1)} %get-tuple-element.75), custom_call_target="InvertDiagBlocksLowerTriangular" | custom-call | tf_op jit(solution)/shard_map/jit(_solve_triangular)/triangular_solve | solution.py:13
  864.3 4.3 while.20
  864.9 1.4 dynamic-slice.64
  867.1 1.4 dynamic-slice.64
  868.6 19.7 %custom-call.28 = f32[2,128,128]{1,2,0:T(8,128)S(1)} custom-call(f32[2,128,128]{2,1,0:T(8,128)S(1)} %get-tuple-element.76), custom_call_target="InvertDiagBlocksLowerTriangular" | custom-call | tf_op jit(solution)/shard_map/jit(_solve_triangular)/triangular_solve | solution.py:17
  890.1 339.9 %all-gather.2 = bf16[256,1,256]{2,1,0:T(2,128)(2,1)S(1)} all-gather(bf16[1,1,256]{2,1,0:T(2,128)(2,1)S(1)} %reshape.430), channel_id=1, replica_groups=mesh['mem'=16,'col'=16] {'mem','col'}, dimensions={0}, use_global_device_ids=true | all-gather | bytes 131584 | tf_op jit(solution)/shard_map/all_gather | solution.py:59
  1230.0 1.2 gather_fusion.2
  1231.6 11.7 cholesky.282
  1243.4 9.8 custom-call.29
  1253.7 11.9 cholesky.299
  1268.6 4.1 while.21
  1269.2 1.3 dynamic-slice.66
  1271.2 1.3 dynamic-slice.66
  1272.7 19.7 %custom-call.30 = f32[2,128,128]{1,2,0:T(8,128)S(1)} custom-call(f32[2,128,128]{2,1,0:T(8,128)S(1)} %get-tuple-element.77), custom_call_target="InvertDiagBlocksLowerTriangular" | custom-call | tf_op jit(solution)/shard_map/jit(_solve_triangular)/triangular_solve | solution.py:13
  1293.3 4.2 while.22
  1293.9 1.4 dynamic-slice.68
  1296.0 1.4 dynamic-slice.68
  1297.5 19.7 %custom-call.31 = f32[2,128,128]{1,2,0:T(8,128)S(1)} custom-call(f32[2,128,128]{2,1,0:T(8,128)S(1)} %get-tuple-element.78), custom_call_target="InvertDiagBlocksLowerTriangular" | custom-call | tf_op jit(solution)/shard_map/jit(_solve_triangular)/triangular_solve | solution.py:17
  1319.0 341.1 %all-gather.3 = bf16[256,1,256]{2,1,0:T(2,128)(2,1)S(1)} all-gather(bf16[1,1,256]{2,1,0:T(2,128)(2,1)S(1)} %reshape.432), channel_id=1, replica_groups=mesh['mem'=16,'col'=16] {'mem','col'}, dimensions={0}, use_global_device_ids=true | all-gather | bytes 131584 | tf_op jit(solution)/shard_map/all_gather | solution.py:59
  1660.1 1.2 gather_fusion.3
  1661.7 11.7 cholesky.316
  1673.5 9.8 custom-call.32
  1683.8 11.9 cholesky.333
  1696.2 0.7 compare_reduce_fusion
  1698.9 4.2 while.23
  1699.5 1.4 dynamic-slice.70
  1701.6 1.4 dynamic-slice.70
  1703.1 19.7 %custom-call.33 = f32[2,128,128]{1,2,0:T(8,128)S(1)} custom-call(f32[2,128,128]{2,1,0:T(8,128)S(1)} %get-tuple-element.79), custom_call_target="InvertDiagBlocksLowerTriangular" | custom-call | tf_op jit(solution)/shard_map/jit(_solve_triangular)/triangular_solve | solution.py:13
  1723.7 4.1 while.24
  1724.4 1.3 dynamic-slice.72
  1726.4 1.3 dynamic-slice.72
  1727.8 19.7 %custom-call.34 = f32[2,128,128]{1,2,0:T(8,128)S(1)} custom-call(f32[2,128,128]{2,1,0:T(8,128)S(1)} %get-tuple-element.80), custom_call_target="InvertDiagBlocksLowerTriangular" | custom-call | tf_op jit(solution)/shard_map/jit(_solve_triangular)/triangular_solve | solution.py:17
  1749.6 1.0 reduce.20
  1751.0 24.1 %all_to_all.30 = bf16[16,2,8192]{2,1,0:T(2,128)(2,1)S(1)} all-to-all(bf16[16,2,8192]{2,1,0:T(2,128)(2,1)S(1)} %reshape.458), channel_id=1, replica_groups=mesh['mem'=16,'col'=16] {'mem'}, dimensions={0} | all-to-all | bytes 1048576 | tf_op jit(solution)/shard_map/all_to_all | solution.py:66
  1775.8 0.8 copy.265
  (213 shorter events, 32.9 us)
Async XLA Ops:
  1.9 9.7 copy-start
  1.9 26.9 %all-to-all-start = ((bf16[16,16,1024]{2,0,1:T(8,128)(2,1)}), bf16[16,16,1024]{2,0,1:T(8,128)(2,1)S(1)}, u32[]{:S(2)}, u32[]{:S(2)}) async-start(bf16[16,16,1024]{2,0,1:T(8,128)(2,1)} %bitcast.243), calls=%async_computation | async-start | bytes 1048576 | tf_op jit(solution)/shard_map/all_to_all | solution.py:48
  20.8 0.7 copy-start.1
where the time goes:
time: 1790 us; the launch traced here: 1780 us
  blocking collectives  1390 us (78%)
  other arithmetic  301 us (17%)
  local copies, waits for them, and re-layouts  44.3 us (2%)
    all_gather x4, blocking collectives, on_device(): everyone = lax.all_gather(owned_cols, ('mem', 'col'), axis=1, tiled=True)  1360 us
    another operation x28, other arithmetic, transform_matrix(): factor = jnp.linalg.cholesky(innov_cov)  139 us
    another operation x9, other arithmetic, transform_matrix(): jax.scipy.linalg.solve_triangular(shifted, first_solve, trans=1, lower=True)  78.9 us
    another operation x4, other arithmetic, transform_matrix(): jax.scipy.linalg.solve_triangular(factor, observed.T.astype(jnp.float32),...  78.7 us
  transfers between devices with their start and end apart: 1, of which 1 were waited for; matrix products, arithmetic and copies ran while one was open for 0% of the time, Pallas kernels for 0%

commit v1 on v0

v1 whole, which is shorter than its diff:
```python
import jax
import jax.numpy as jnp
from jax import lax
from jax.experimental import pallas as pl
from jax.experimental.pallas import tpu as pltpu
from jax.sharding import PartitionSpec as P

F32 = jnp.float32
BF16 = jnp.bfloat16
STEPS = 4
RESIDUAL_MAX = 4e-3
PAD = 128


def mul(a, b):
    return lax.dot_general(
        a.astype(BF16), b.astype(BF16), (((1,), (0,)), ((), ())), preferred_element_type=F32
    )


def mul_t(a, b):
    return lax.dot_general(
        a.astype(BF16), b.astype(BF16), (((1,), (1,)), ((), ())), preferred_element_type=F32
    )


def iotas(n):
    rows = lax.broadcasted_iota(jnp.int32, (n, n), 0)
    cols = lax.broadcasted_iota(jnp.int32, (n, n), 1)
    return rows, cols


def fast_transform(obs, obs_t, var_row, var_col, inverse_count):
    n = obs.shape[1]
    rows, cols = iotas(n)
    wide = obs.astype(F32)
    wide_t = obs_t.astype(F32)
    dr = lax.rsqrt(jnp.sum(wide * wide, axis=0, keepdims=True) * inverse_count + var_row)
    dc = lax.rsqrt(jnp.sum(wide_t * wide_t, axis=1, keepdims=True) * inverse_count + var_col)
    gram = mul_t(obs_t, obs_t)
    error = jnp.where(rows == cols, 0.0, gram * (dc * inverse_count) * dr)
    lower = jnp.where(rows > cols, 1.0, jnp.where(rows == cols, 0.5, 0.0))
    first_t = wide * (dr * (inverse_count**0.5))
    factor = None
    for step in range(STEPS):
        f = error * lower
        half = f.astype(BF16)
        if step == 0:
            factor = jnp.where(rows == cols, 1.0, 0.0) - f
        else:
            factor = factor - mul(half, factor)
        first_t = first_t - mul_t(first_t, half)
        if step < STEPS - 1:
            y = (error - f) - mul(half, error)
            error = y - (error - f) - mul_t(y, half)
    left = jnp.sum(error * error)
    x = jnp.sqrt(var_row) * dr
    diagonal = jnp.sum(jnp.where(rows == cols, factor, 0.0), axis=0, keepdims=True) * x
    scale = 1.0 / (1.0 + diagonal)
    b = jnp.where(rows > cols, factor * (x * scale), 0.0)
    b2 = mul(b, b)
    second_t = first_t * scale
    second_t = second_t - mul(second_t, b)
    b4 = mul(b2, b2)
    second_t = second_t + mul(second_t, b2)
    second_t = second_t + mul(second_t, b4)
    left = jnp.maximum(left, jnp.sum(b4 * b4))
    product = mul_t(first_t, second_t)
    transform = jnp.where(rows == cols, 1.0, 0.0) - product
    return transform.astype(BF16), left


def exact(a, b, dims):
    return lax.dot_general(
        a, b, (dims, ((), ())), precision=lax.Precision.HIGHEST, preferred_element_type=F32
    )


def slow_transform(obs, obs_t, var_row, cov_ref, inv_ref, shift_ref, inverse_count):
    n = obs.shape[1]
    rows, cols = iotas(n)
    on_diagonal = rows == cols
    gram = mul_t(obs_t, obs_t) * inverse_count
    cov_ref[...] = gram + jnp.where(on_diagonal, var_row, 0.0)
    inv_ref[...] = jnp.where(on_diagonal, 1.0, 0.0)
    shift_ref[...] = jnp.where(on_diagonal, 1.0, 0.0)
    lane = lax.broadcasted_iota(jnp.int32, (1, n), 1)
    sublane = lax.broadcasted_iota(jnp.int32, (n, 1), 0)

    def eliminate(j, carry):
        cov = cov_ref[...]
        cov_row = cov_ref[pl.ds(j, 1), :]
        column = jnp.sum(jnp.where(cols == j, cov, 0.0), axis=1, keepdims=True)
        pivot = jnp.sum(jnp.where(lane == j, cov_row, 0.0), axis=1, keepdims=True)
        noise = jnp.sum(jnp.where(lane == j, var_row, 0.0), axis=1, keepdims=True)
        root = jnp.sqrt(pivot)
        below = jnp.where(sublane > j, column / root, 0.0)
        inv_row = inv_ref[pl.ds(j, 1), :] / root
        shift_row = shift_ref[pl.ds(j, 1), :] / (root + jnp.sqrt(noise))
        cov_ref[...] = cov - below * (cov_row / root)
        inv_ref[...] = jnp.where(sublane == j, inv_row, inv_ref[...] - below * inv_row)
        shift_ref[...] = jnp.where(sublane == j, shift_row, shift_ref[...] - below * shift_row)
        return carry

    lax.fori_loop(0, n, eliminate, 0)
    first_t = exact(obs.astype(F32), inv_ref[...], ((1,), (1,)))
    second_t = exact(first_t, shift_ref[...], ((1,), (0,)))
    product = exact(obs.astype(F32), second_t, ((1,), (1,)))
    transform = jnp.where(on_diagonal, 1.0, 0.0) - product * inverse_count
    return transform.astype(BF16)


def transform_kernel(
    seen_ref, index_ref, var_ref, var_col_ref, weights_ref,
    obs_ref, obs_t_ref, cov_ref, inv_ref, shift_ref, *, block_cols, inverse_count
):
    batches, observations = var_ref.shape
    per_batch = seen_ref.shape[1] // batches
    rows, cols = iotas(observations)
    eye = jnp.where(rows == cols, 1.0, 0.0).astype(BF16)

    def load():
        for batch in range(batches):
            place = index_ref[:, batch : batch + 1] // block_cols
            order = jnp.where(cols == place, 1.0, 0.0)
            seen = seen_ref[:, batch * per_batch : (batch + 1) * per_batch, :]
            obs_t = mul(order, seen.reshape(observations, seen.shape[2])).astype(BF16)
            obs_t_ref[batch] = obs_t
            obs_ref[batch] = mul_t(eye, obs_t).astype(BF16)

    def advance(weights, batch):
        weights_ref[batch] = weights
        for later in range(batch + 1, batches):
            obs = obs_ref[later]
            obs_t = obs_t_ref[later]
            obs_ref[later] = mul(weights, obs).astype(BF16)
            obs_t_ref[later] = mul_t(obs_t, weights).astype(BF16)

    load()
    left = jnp.float32(0.0)
    for batch in range(batches):
        weights, part = fast_transform(
            obs_ref[batch], obs_t_ref[batch], var_ref[batch : batch + 1, :],
            var_col_ref[:, batch : batch + 1], inverse_count,
        )
        left = jnp.maximum(left, part)
        advance(weights, batch)

    @pl.when(jnp.logical_not(left <= RESIDUAL_MAX))
    def _():
        load()
        for batch in range(batches):
            weights = slow_transform(
                obs_ref[batch], obs_t_ref[batch], var_ref[batch : batch + 1, :],
                cov_ref, inv_ref, shift_ref, inverse_count,
            )
            advance(weights, batch)


def transforms(seen, index, var, members, block_cols):
    batches, observations = var.shape
    square = (observations, observations)
    return pl.pallas_call(
        lambda *refs: transform_kernel(
            *refs, block_cols=block_cols, inverse_count=1.0 / (members - 1)
        ),
        out_shape=jax.ShapeDtypeStruct((batches, members, members), BF16),
        in_specs=[pl.BlockSpec(memory_space=pltpu.VMEM)] * 4,
        out_specs=pl.BlockSpec(memory_space=pltpu.VMEM),
        scratch_shapes=[
            pltpu.VMEM((batches, members, observations), BF16),
            pltpu.VMEM((batches, observations, members), BF16),
            pltpu.VMEM(square, F32),
            pltpu.VMEM(square, F32),
            pltpu.VMEM(square, F32),
        ],
        compiler_params=pltpu.CompilerParams(vmem_limit_bytes=32 << 20),
        cost_estimate=pl.CostEstimate(flops=8 * 10**9, bytes_accessed=1 << 20, transcendentals=0),
        name="transforms",
    )(seen, index.T, var, var.T)


def apply_kernel(weights_ref, block_ref, out_ref):
    batches = weights_ref.shape[0]
    columns = out_ref.shape[1]
    chunk = min(columns, 512)
    for start in range(0, columns, chunk):
        piece = slice(start, start + chunk)
        part = block_ref[:, piece]
        for batch in range(batches):
            part = mul(weights_ref[batch], part).astype(BF16)
        out_ref[:, piece] = part


def apply(weights, block):
    return pl.pallas_call(
        apply_kernel,
        out_shape=jax.ShapeDtypeStruct(block.shape, BF16),
        in_specs=[pl.BlockSpec(memory_space=pltpu.VMEM)] * 2,
        out_specs=pl.BlockSpec(memory_space=pltpu.VMEM),
        compiler_params=pltpu.CompilerParams(vmem_limit_bytes=16 << 20),
        name="apply",
    )(weights, block)


def select_kernel(first_ref, block_ref, index_ref, seen_ref, *, block_cols):
    batches = index_ref.shape[0]
    members, group_cols = block_ref.shape
    blocks = group_cols // block_cols
    local = index_ref[...] - first_ref[0]
    lane = lax.broadcasted_iota(jnp.int32, (1, block_cols), 1)
    slot = lax.broadcasted_iota(jnp.int32, (1, PAD), 1)
    seen = jnp.zeros((members, PAD), F32)
    for block in range(blocks):
        inside = local - block * block_cols
        inside = jnp.where((inside >= 0) & (inside < block_cols), inside, 0).astype(F32)
        offsets = jnp.sum(inside, axis=1, keepdims=True).astype(jnp.int32)
        values = block_ref[:, block * block_cols : (block + 1) * block_cols].astype(F32)
        for batch in range(batches):
            chosen = jnp.where(lane == offsets[batch : batch + 1, :], values, 0.0)
            column = jnp.sum(chosen, axis=1, keepdims=True)
            seen = jnp.where(slot == batch * blocks + block, column, seen)
    seen = seen.astype(BF16)
    for peer in range(seen_ref.shape[0]):
        seen_ref[peer] = seen


def select(perturbations, index, first, block_cols, peers):
    members = perturbations.shape[0]
    return pl.pallas_call(
        lambda *refs: select_kernel(*refs, block_cols=block_cols),
        out_shape=jax.ShapeDtypeStruct((peers, members, PAD), BF16),
        in_specs=[pl.BlockSpec(memory_space=pltpu.SMEM)]
        + [pl.BlockSpec(memory_space=pltpu.VMEM)] * 2,
        out_specs=pl.BlockSpec(memory_space=pltpu.VMEM),
        compiler_params=pltpu.CompilerParams(vmem_limit_bytes=16 << 20),
        name="select",
    )(first.reshape(1), perturbations, index)


def on_device(perturbations, obs_index, obs_var):
    members_here, group_cols = perturbations.shape
    mem_count = lax.axis_size("mem")
    col_count = lax.axis_size("col")
    members = members_here * mem_count
    block_cols = group_cols // mem_count
    batches = obs_index.shape[0]
    owned = batches * mem_count
    first = lax.axis_index("col").astype(jnp.int32) * group_cols
    sent = select(perturbations, obs_index, first, block_cols, mem_count)
    seen_group = lax.all_to_all(sent, "mem", split_axis=0, concat_axis=0, tiled=True)
    arranged = perturbations.reshape(members_here, mem_count, block_cols).transpose(1, 0, 2)
    arranged, seen_group = lax.optimization_barrier((arranged, seen_group))
    block = lax.all_to_all(arranged, "mem", split_axis=0, concat_axis=0, tiled=True)
    block = block.reshape(members, block_cols)
    seen_group = seen_group.reshape(members, PAD)[:, :owned].T
    seen = lax.all_to_all(
        jnp.broadcast_to(seen_group, (col_count, owned, members)),
        "col", split_axis=0, concat_axis=0, tiled=True,
    )
    weights = transforms(seen, obs_index, obs_var, members, block_cols)
    ensemble = apply(weights, block)
    returned = lax.all_to_all(
        ensemble.reshape(mem_count, members_here, block_cols), "mem",
        split_axis=0, concat_axis=0, tiled=True,
    )
    return returned.transpose(1, 0, 2).reshape(members_here, group_cols)


def solution(mesh):
    return jax.shard_map(
        on_device,
        mesh=mesh,
        in_specs=(P("mem", "col"), P(), P()),
        out_specs=P("mem", "col"),
        check_vma=False,
    )
```

time: 1790 us -> 290 us (0.16)
  blocking collectives: 1390 us -> 42.3 us
  other arithmetic: 301 us -> 0 us
  Pallas kernels: 0 us -> 221 us
  local copies, waits for them, and re-layouts: 44.3 us -> 4.34 us
    all_gather x4 -> x0, blocking collectives: 1360 us -> none  [on_device(): everyone = lax.all_gather(owned_cols, ('mem', 'col'), axis=1, tiled=True)]
    another operation x41 -> x0, other arithmetic: 297 us -> none  [the longest x28 139 us: transform_matrix(): factor = jnp.linalg.cholesky(innov_cov)]
    pallas_call x0 -> x3, Pallas kernels: none -> 221 us  [the longest x1 218 us: transforms(): pl.pallas_call(lambda *refs: transform_kernel(*refs, block_cols=block_col...]
    another operation x117 -> x0, local copies, waits for them, and re-layouts: 34 us -> none  [the longest x49 16.6 us: transform_matrix(): jax.scipy.linalg.solve_triangular(shifted, first_solve, trans=1, lower=True)]
    all_to_all x1 -> x2, blocking collectives: 24.1 us -> 42.3 us  [the longest x1 26.6 us: on_device(): lax.all_to_all(ensemble.reshape(mem_count, members_here, block_cols), 'me...]
  transfers between devices with their start and end apart: 1 -> 2, of which waited for: 1 -> 1; matrix products, arithmetic and copies ran while one was open for 0% -> 0% of each run, Pallas kernels for 0% -> 75%
where the time goes in v1:
time: 290 us; the launch traced here: 289 us
  Pallas kernels  221 us (76%)
  blocking collectives  42.3 us (15%)
  starting transfers between devices  13.2 us (5%)
  waiting for transfers between devices  8.2 us (3%)
  local copies, waits for them, and re-layouts  4.34 us (1%)
    pallas_call x1, Pallas kernels, transforms(): pl.pallas_call(lambda *refs: transform_kernel(*refs, block_cols=block_col...  218 us
    all_to_all x1, blocking collectives, on_device(): lax.all_to_all(ensemble.reshape(mem_count, members_here, block_cols), 'me...  26.6 us
    all_to_all x1, blocking collectives, on_device(): lax.all_to_all(jnp.broadcast_to(seen_group, (col_count, owned, members)),...  15.7 us
    all_to_all x1, starting transfers between devices, on_device(): lax.all_to_all(sent, 'mem', split_axis=0, concat_axis=0, tiled=True)  9.58 us
    all_to_all x1, waiting for transfers between devices, on_device(): lax.all_to_all(sent, 'mem', split_axis=0, concat_axis=0, tiled=True)  8.2 us
  transfers between devices with their start and end apart: 2, of which 1 were waited for; matrix products, arithmetic and copies ran while one was open for 0% of the time, Pallas kernels for 75%

profile of v1, /device:TPU:2, one launch (start us, length us, event | category | flops | bytes accessed | tf_op | source)
XLA Modules:
  0.0 289.4 jit_solution(13303518407852039978)
XLA Ops:
  0.0 0.0 copy-start.2
  0.0 0.7 copy-done.2
  0.7 0.0 copy-start
  0.7 1.0 copy-done
  1.7 0.0 copy-start.1
  1.7 1.4 select.1
  3.1 9.6 %all-to-all-start = ((bf16[16,16,128]{2,1,0:T(8,128)(2,1)}), bf16[16,16,128]{2,1,0:T(8,128)(2,1)S(1)}, u32[]{:S(2)}, u32[]{:S(2)}) async-start(bf16[16,16,128]{2,1,0:T(8,128)(2,1)} %select.1), calls=%async_computation | async-start | bytes 131072 | tf_op jit(solution)/shard_map/all_to_all | solution.py:251
  12.7 0.0 copy-done.1
  12.7 0.8 copy.13
  13.5 8.2 %all-to-all-done = bf16[16,16,128]{2,1,0:T(8,128)(2,1)S(1)} async-done(((bf16[16,16,128]{2,1,0:T(8,128)(2,1)}), bf16[16,16,128]{2,1,0:T(8,128)(2,1)S(1)}, u32[]{:S(2)}, u32[]{:S(2)}) %all-to-all-start) | async-done | bytes 65568 | tf_op jit(solution)/shard_map/all_to_all | solution.py:251
  21.7 0.1 copy.9
  21.9 15.7 %all_to_all.20.refs_0_ = bf16[16,64,256]{2,1,0:T(8,128)(2,1)S(1)} all-to-all(bf16[16,64,256]{2,1,0:T(8,128)(2,1)S(1)} %broadcast_in_dim.3), channel_id=1, replica_groups=mesh['mem'=16,'col'=16] {'col'}, dimensions={0} | all-to-all | bytes 1048576 | tf_op jit(solution)/shard_map/all_to_all | solution.py:257
  37.6 3.6 %all-to-all-start.2 = ((bf16[16,16,1024]{2,1,0:T(8,128)(2,1)}), bf16[16,16,1024]{2,1,0:T(8,128)(2,1)S(1)}, u32[]{:S(2)}, u32[]{:S(2)}) async-start(bf16[16,16,1024]{2,1,0:T(8,128)(2,1)} %bitcast.16), calls=%async_computation.2 | async-start | bytes 1048576 | tf_op jit(solution)/shard_map/all_to_all | solution.py:254
  41.2 0.0 copy-start.3
  41.2 0.1 copy.6
  41.3 0.5 copy-done.3
  41.9 0.1 copy.7
  42.0 218.5 %transforms.1.weights_ref = bf16[4,256,256]{2,1,0:T(8,128)(2,1)S(1)} custom-call(bf16[16,64,256]{2,1,0:T(8,128)(2,1)S(1)} %all_to_all.20.refs_0_, s32[256,4]{1,0:T(8,128)S(1)} %bitcast.21, f32[4,256]{1,0:T(4,128)S(1)} %copy-done.3, f32[256,4]{1,0:T(8,128)S(1)} %bitcast.22), custom_call_target="tpu_custom_call" | custom-call | flops 8000000000 | bytes 1048576 | tf_op jit(solution)/shard_map/transforms/pallas_call | solution.py:163
  260.5 0.0 all-to-all-done.2
  260.5 1.5 apply.1
  262.0 26.6 %all_to_all.21 = bf16[16,16,1024]{2,1,0:T(8,128)(2,1)S(1)} all-to-all(bf16[16,16,1024]{2,1,0:T(8,128)(2,1)S(1)} %bitcast.19), channel_id=1, replica_groups=mesh['mem'=16,'col'=16] {'mem'}, dimensions={0} | all-to-all | bytes 1048576 | tf_op jit(solution)/shard_map/all_to_all | solution.py:263
  288.6 0.8 copy.11
  (1 shorter events, 0.0 us)
Async XLA Ops:
  0.0 0.7 copy-start.2
  0.7 1.0 copy-start
  1.7 11.0 %copy-start.1 = (bf16[16,16384]{1,0:T(8,128)(2,1)S(1)}, bf16[16,16384]{1,0:T(8,128)(2,1)}, u32[]{:S(2)}) copy-start(bf16[16,16384]{1,0:T(8,128)(2,1)} %refs_1_.1) | copy-start | bytes 1572868
  3.1 18.6 %all-to-all-start = ((bf16[16,16,128]{2,1,0:T(8,128)(2,1)}), bf16[16,16,128]{2,1,0:T(8,128)(2,1)S(1)}, u32[]{:S(2)}, u32[]{:S(2)}) async-start(bf16[16,16,128]{2,1,0:T(8,128)(2,1)} %select.1), calls=%async_computation | async-start | bytes 131072 | tf_op jit(solution)/shard_map/all_to_all | solution.py:251
  37.6 222.9 %all-to-all-start.2 = ((bf16[16,16,1024]{2,1,0:T(8,128)(2,1)}), bf16[16,16,1024]{2,1,0:T(8,128)(2,1)S(1)}, u32[]{:S(2)}, u32[]{:S(2)}) async-start(bf16[16,16,1024]{2,1,0:T(8,128)(2,1)} %bitcast.16), calls=%async_computation.2 | async-start | bytes 1048576 | tf_op jit(solution)/shard_map/all_to_all | solution.py:254
  41.2 0.7 copy-start.3

commit v2 on v1

--- a/solution.py
+++ b/solution.py
@@ -111,20 +111,23 @@
 
 
 def transform_kernel(
-    seen_ref, index_ref, var_ref, var_col_ref, weights_ref,
-    obs_ref, obs_t_ref, cov_ref, inv_ref, shift_ref, *, block_cols, inverse_count
+    near_ref, far_ref, place_ref, var_ref, var_col_ref, weights_ref,
+    obs_ref, obs_t_ref, cov_ref, inv_ref, shift_ref, *, inverse_count
 ):
     batches, observations = var_ref.shape
-    per_batch = seen_ref.shape[1] // batches
+    pieces, rows_held, members = near_ref.shape
+    per_batch = rows_held // batches
+    half = pieces * per_batch
     rows, cols = iotas(observations)
     eye = jnp.where(rows == cols, 1.0, 0.0).astype(BF16)
 
     def load():
         for batch in range(batches):
-            place = index_ref[:, batch : batch + 1] // block_cols
-            order = jnp.where(cols == place, 1.0, 0.0)
-            seen = seen_ref[:, batch * per_batch : (batch + 1) * per_batch, :]
-            obs_t = mul(order, seen.reshape(observations, seen.shape[2])).astype(BF16)
+            order = jnp.where(cols == place_ref[:, batch : batch + 1], 1.0, 0.0)
+            held = slice(batch * per_batch, (batch + 1) * per_batch)
+            near = near_ref[:, held, :].reshape(half, members)
+            far = far_ref[:, held, :].reshape(half, members)
+            obs_t = mul(order, jnp.concatenate([near, far])).astype(BF16)
             obs_t_ref[batch] = obs_t
             obs_ref[batch] = mul_t(eye, obs_t).astype(BF16)
 
@@ -157,15 +160,15 @@
             advance(weights, batch)
 
 
-def transforms(seen, index, var, members, block_cols):
+def transforms(near, far, place, var, members):
     batches, observations = var.shape
     square = (observations, observations)
     return pl.pallas_call(
         lambda *refs: transform_kernel(
-            *refs, block_cols=block_cols, inverse_count=1.0 / (members - 1)
+            *refs, inverse_count=1.0 / (members - 1)
         ),
         out_shape=jax.ShapeDtypeStruct((batches, members, members), BF16),
-        in_specs=[pl.BlockSpec(memory_space=pltpu.VMEM)] * 4,
+        in_specs=[pl.BlockSpec(memory_space=pltpu.VMEM)] * 5,
         out_specs=pl.BlockSpec(memory_space=pltpu.VMEM),
         scratch_shapes=[
             pltpu.VMEM((batches, members, observations), BF16),
@@ -177,7 +180,7 @@
         compiler_params=pltpu.CompilerParams(vmem_limit_bytes=32 << 20),
         cost_estimate=pl.CostEstimate(flops=8 * 10**9, bytes_accessed=1 << 20, transcendentals=0),
         name="transforms",
-    )(seen, index.T, var, var.T)
+    )(near, far, place.T, var, var.T)
 
 
 def apply_kernel(weights_ref, block_ref, out_ref):
@@ -236,6 +239,19 @@
         compiler_params=pltpu.CompilerParams(vmem_limit_bytes=16 << 20),
         name="select",
     )(first.reshape(1), perturbations, index)
+
+
+def swapped(value, bits, count):
+    return lax.ppermute(value, "col", [(i, i ^ bits) for i in range(count)])
+
+
+def gather_col(own, count):
+    pair = jnp.concatenate([own, swapped(own, 8, count)])
+    half = jnp.concatenate([pair] + [swapped(pair, bits, count) for bits in (2, 6, 4)])
+    return half, swapped(half, 1, count)
+
+
+PIECES = [p ^ q ^ r for r in (0, 1) for q in (0, 2, 6, 4) for p in (0, 8)]
 
 
 def on_device(perturbations, obs_index, obs_var):
@@ -254,11 +270,11 @@
     block = lax.all_to_all(arranged, "mem", split_axis=0, concat_axis=0, tiled=True)
     block = block.reshape(members, block_cols)
     seen_group = seen_group.reshape(members, PAD)[:, :owned].T
-    seen = lax.all_to_all(
-        jnp.broadcast_to(seen_group, (col_count, owned, members)),
-        "col", split_axis=0, concat_axis=0, tiled=True,
-    )
-    weights = transforms(seen, obs_index, obs_var, members, block_cols)
+    near, far = gather_col(seen_group[None], col_count)
+    away = (obs_index // group_cols) ^ lax.axis_index("col").astype(jnp.int32)
+    piece = sum(jnp.where(away == p, at, 0) for at, p in enumerate(PIECES))
+    place = piece * mem_count + obs_index % group_cols // block_cols
+    weights = transforms(near, far, place, obs_var, members)
     ensemble = apply(weights, block)
     returned = lax.all_to_all(
         ensemble.reshape(mem_count, members_here, block_cols), "mem",

time: 290 us -> 286 us (0.986)
  blocking collectives: 42.3 us -> 26.1 us
  starting transfers between devices: 13.2 us -> 21 us
    all_to_all x1 -> x0, blocking collectives: 15.7 us -> none  [on_device(): lax.all_to_all(jnp.broadcast_to(seen_group, (col_count, owned, members)),...]
    ppermute x0 -> x5, starting transfers between devices: none -> 7.87 us  [swapped(): return lax.ppermute(value, 'col', [(i, i ^ bits) for i in range(count)])]
  transfers between devices with their start and end apart: 2 -> 7, of which waited for: 1 -> 3; matrix products, arithmetic and copies ran while one was open for 0% -> 1% of each run, Pallas kernels for 75% -> 77%
where the time goes in v2:
time: 286 us; the launch traced here: 285 us
  Pallas kernels  222 us (78%)
  blocking collectives  26.1 us (9%)
  starting transfers between devices  21 us (7%)
  waiting for transfers between devices  10.6 us (4%)
  local copies, waits for them, and re-layouts  4.46 us (2%)
    pallas_call x1, Pallas kernels, transforms(): pl.pallas_call(lambda *refs: transform_kernel(*refs, inverse_count=1.0 /...  219 us
    all_to_all x1, blocking collectives, on_device(): lax.all_to_all(ensemble.reshape(mem_count, members_here, block_cols), 'me...  26.1 us
    all_to_all x1, starting transfers between devices, on_device(): lax.all_to_all(sent, 'mem', split_axis=0, concat_axis=0, tiled=True)  9.58 us
    all_to_all x1, waiting for transfers between devices, on_device(): lax.all_to_all(sent, 'mem', split_axis=0, concat_axis=0, tiled=True)  8.2 us
    ppermute x5, starting transfers between devices, swapped(): return lax.ppermute(value, 'col', [(i, i ^ bits) for i in range(count)])  7.87 us
  transfers between devices with their start and end apart: 7, of which 3 were waited for; matrix products, arithmetic and copies ran while one was open for 1% of the time, Pallas kernels for 77%

profile of v2, /device:TPU:2, one launch (start us, length us, event | category | flops | bytes accessed | tf_op | source)
XLA Modules:
  0.0 284.9 jit_solution(16702018905419587743)
XLA Ops:
  0.0 0.0 copy-start.2
  0.0 0.7 copy-done.2
  0.7 0.0 copy-start
  0.7 1.0 copy-done
  1.7 0.0 copy-start.1
  1.7 1.4 select.11
  3.1 9.6 %all-to-all-start = ((bf16[16,16,128]{2,1,0:T(8,128)(2,1)}), bf16[16,16,128]{2,1,0:T(8,128)(2,1)S(1)}, u32[]{:S(2)}, u32[]{:S(2)}) async-start(bf16[16,16,128]{2,1,0:T(8,128)(2,1)} %select.11), calls=%async_computation | async-start | bytes 131072 | tf_op jit(solution)/shard_map/all_to_all | solution.py:267
  12.7 0.0 copy-done.1
  12.7 0.8 copy.30
  13.6 8.2 %all-to-all-done = bf16[16,16,128]{2,1,0:T(8,128)(2,1)S(1)} async-done(((bf16[16,16,128]{2,1,0:T(8,128)(2,1)}), bf16[16,16,128]{2,1,0:T(8,128)(2,1)S(1)}, u32[]{:S(2)}, u32[]{:S(2)}) %all-to-all-start) | async-done | bytes 65568 | tf_op jit(solution)/shard_map/all_to_all | solution.py:267
  21.8 0.1 copy.26
  21.9 3.0 %collective-permute-start = (bf16[1,64,256]{2,1,0:T(8,128)(2,1)S(1)}, bf16[1,64,256]{2,1,0:T(8,128)(2,1)S(1)}, u32[]{:S(2)}, u32[]{:S(2)}) collective-permute-start(bf16[1,64,256]{2,1,0:T(8,128)(2,1)S(1)} %bitcast.27), channel_id=1, source_target_pairs={{0,8},{1,9},{2,10},{3,11},{4,12},{5,13},{6,14},{7,15},{8,0},{9,1},... | collective-permute-start | bytes 98312 | tf_op jit(solution)/shard_map/ppermute | solution.py:245
  24.8 3.6 %all-to-all-start.1 = ((bf16[16,16,1024]{2,1,0:T(8,128)(2,1)}), bf16[16,16,1024]{2,1,0:T(8,128)(2,1)S(1)}, u32[]{:S(2)}, u32[]{:S(2)}) async-start(bf16[16,16,1024]{2,1,0:T(8,128)(2,1)} %bitcast.20), calls=%async_computation.1 | async-start | bytes 1048576 | tf_op jit(solution)/shard_map/all_to_all | solution.py:270
  28.4 0.0 collective-permute-done
  28.5 2.2 collective-permute-start.3
  30.7 0.0 collective-permute-start.2
  30.7 2.6 collective-permute-start.1
  33.2 2.2 collective-permute-done.1
  35.5 0.0 collective-permute-done.2
  35.5 0.0 collective-permute-done.3
  35.5 0.1 collective-permute-start.4
  35.7 0.1 copy.17
  35.8 0.0 copy-start.3
  35.8 0.2 copy.22
  36.0 0.5 copy-done.3
  36.5 0.1 copy.24
  36.6 0.4 fusion.3.refs_2_
  37.0 0.1 collective-permute-done.4.refs_1_
  37.2 219.3 %transforms.1.weights_ref = bf16[4,256,256]{2,1,0:T(8,128)(2,1)S(1)} custom-call(bf16[8,64,256]{2,1,0:T(8,128)(2,1)S(1)} %constant_dynamic-update-slice_fusion.refs_0_, bf16[8,64,256]{2,1,0:T(8,128)(2,1)S(1)} %collective-permute-done.4.refs_1_, s32[256,4]{1,0:T(8,128)S(1)} %fusion.3.refs_2_, f32[4,256]{1,0:T(4,128)S(1)} %copy-done.3, f32[256,4]{1,0:T(8,128)S(1)} %bitcast.25), custom_call_target="tpu_custom_call" | custom-call | flops 8000000000 | bytes 1048576 | tf_op jit(solution)/shard_map/transforms/pallas_call | solution.py:166
  256.4 0.0 all-to-all-done.1
  256.4 1.5 apply.1
  257.9 26.1 %all_to_all.15 = bf16[16,16,1024]{2,1,0:T(8,128)(2,1)S(1)} all-to-all(bf16[16,16,1024]{2,1,0:T(8,128)(2,1)S(1)} %bitcast.23), channel_id=1, replica_groups=mesh['mem'=16,'col'=16] {'mem'}, dimensions={0} | all-to-all | bytes 1048576 | tf_op jit(solution)/shard_map/all_to_all | solution.py:279
  284.1 0.8 copy.28
  (7 shorter events, 0.0 us)
Async XLA Ops:
  0.0 0.7 copy-start.2
  0.7 1.0 copy-start
  1.7 11.0 %copy-start.1 = (bf16[16,16384]{1,0:T(8,128)(2,1)S(1)}, bf16[16,16384]{1,0:T(8,128)(2,1)}, u32[]{:S(2)}) copy-start(bf16[16,16384]{1,0:T(8,128)(2,1)} %refs_1_.1) | copy-start | bytes 1572868
  3.1 18.6 %all-to-all-start = ((bf16[16,16,128]{2,1,0:T(8,128)(2,1)}), bf16[16,16,128]{2,1,0:T(8,128)(2,1)S(1)}, u32[]{:S(2)}, u32[]{:S(2)}) async-start(bf16[16,16,128]{2,1,0:T(8,128)(2,1)} %select.11), calls=%async_computation | async-start | bytes 131072 | tf_op jit(solution)/shard_map/all_to_all | solution.py:267
  21.9 6.6 %collective-permute-start = (bf16[1,64,256]{2,1,0:T(8,128)(2,1)S(1)}, bf16[1,64,256]{2,1,0:T(8,128)(2,1)S(1)}, u32[]{:S(2)}, u32[]{:S(2)}) collective-permute-start(bf16[1,64,256]{2,1,0:T(8,128)(2,1)S(1)} %bitcast.27), channel_id=1, source_target_pairs={{0,8},{1,9},{2,10},{3,11},{4,12},{5,13},{6,14},{7,15},{8,0},{9,1},... | collective-permute-start | bytes 98312 | tf_op jit(solution)/shard_map/ppermute | solution.py:245
  24.8 231.6 %all-to-all-start.1 = ((bf16[16,16,1024]{2,1,0:T(8,128)(2,1)}), bf16[16,16,1024]{2,1,0:T(8,128)(2,1)S(1)}, u32[]{:S(2)}, u32[]{:S(2)}) async-start(bf16[16,16,1024]{2,1,0:T(8,128)(2,1)} %bitcast.20), calls=%async_computation.1 | async-start | bytes 1048576 | tf_op jit(solution)/shard_map/all_to_all | solution.py:270
  28.5 7.1 %collective-permute-start.3 = (bf16[2,64,256]{2,1,0:T(8,128)(2,1)S(1)}, bf16[2,64,256]{2,1,0:T(8,128)(2,1)S(1)}, u32[]{:S(2)}, u32[]{:S(2)}) collective-permute-start(bf16[2,64,256]{2,1,0:T(8,128)(2,1)S(1)} %pad_maximum_fusion), channel_id=1, source_target_pairs={{0,4},{1,5},{2,6},{3,7},{4,0},{5,1},{6,2},{7,3},{8,12},{9,13},{10,... | collective-permute-start | bytes 196616 | tf_op jit(solution)/shard_map/ppermute | solution.py:245
  30.7 4.8 %collective-permute-start.2 = (bf16[2,64,256]{2,1,0:T(8,128)(2,1)S(1)}, bf16[2,64,256]{2,1,0:T(8,128)(2,1)S(1)}, u32[]{:S(2)}, u32[]{:S(2)}) collective-permute-start(bf16[2,64,256]{2,1,0:T(8,128)(2,1)S(1)} %pad_maximum_fusion), channel_id=1, source_target_pairs={{0,6},{1,7},{2,4},{3,5},{4,2},{5,3},{6,0},{7,1},{8,14},{9,15},{10,... | collective-permute-start | bytes 196616 | tf_op jit(solution)/shard_map/ppermute | solution.py:245
  30.7 4.8 %collective-permute-start.1 = (bf16[2,64,256]{2,1,0:T(8,128)(2,1)S(1)}, bf16[2,64,256]{2,1,0:T(8,128)(2,1)S(1)}, u32[]{:S(2)}, u32[]{:S(2)}) collective-permute-start(bf16[2,64,256]{2,1,0:T(8,128)(2,1)S(1)} %pad_maximum_fusion), channel_id=1, source_target_pairs={{0,2},{1,3},{2,0},{3,1},{4,6},{5,7},{6,4},{7,5},{8,10},{9,11},{10,... | collective-permute-start | bytes 196616 | tf_op jit(solution)/shard_map/ppermute | solution.py:245
  35.5 1.6 collective-permute-start.4
  35.8 0.7 copy-start.3

commit v3 on v2

--- a/solution.py
+++ b/solution.py
@@ -1,3 +1,5 @@
+import math
+
 import jax
 import jax.numpy as jnp
 from jax import lax
@@ -7,8 +9,10 @@
 
 F32 = jnp.float32
 BF16 = jnp.bfloat16
-STEPS = 4
-RESIDUAL_MAX = 4e-3
+START = 0.86
+STRETCH = (1.07, 1.003)
+RESIDUAL_MAX = 3e-2
+B_WEIGHT = 300.0
 PAD = 128
 
 
@@ -30,7 +34,7 @@
     return rows, cols
 
 
-def fast_transform(obs, obs_t, var_row, var_col, inverse_count):
+def fast_transform(obs, obs_t, var_row, var_col, lower_ref, upper_ref, inverse_count):
     n = obs.shape[1]
     rows, cols = iotas(n)
     wide = obs.astype(F32)
@@ -38,36 +42,41 @@
     dr = lax.rsqrt(jnp.sum(wide * wide, axis=0, keepdims=True) * inverse_count + var_row)
     dc = lax.rsqrt(jnp.sum(wide_t * wide_t, axis=1, keepdims=True) * inverse_count + var_col)
     gram = mul_t(obs_t, obs_t)
-    error = jnp.where(rows == cols, 0.0, gram * (dc * inverse_count) * dr)
-    lower = jnp.where(rows > cols, 1.0, jnp.where(rows == cols, 0.5, 0.0))
-    first_t = wide * (dr * (inverse_count**0.5))
+    error = jnp.where(rows == cols, START - 1.0, gram * (dc * (START * inverse_count)) * dr)
+    size = math.sqrt(START * math.prod(STRETCH))
+    first_t = wide * (dr * (size * math.sqrt(inverse_count)))
     factor = None
-    for step in range(STEPS):
-        f = error * lower
-        half = f.astype(BF16)
+    for step in range(len(STRETCH) + 1):
+        near = error.astype(BF16)
+        f = near * lower_ref[...]
         if step == 0:
-            factor = jnp.where(rows == cols, 1.0, 0.0) - f
+            factor = jnp.where(rows == cols, size, 0.0) - size * f.astype(F32)
         else:
-            factor = factor - mul(half, factor)
-        first_t = first_t - mul_t(first_t, half)
-        if step < STEPS - 1:
-            y = (error - f) - mul(half, error)
-            error = y - (error - f) - mul_t(y, half)
-    left = jnp.sum(error * error)
+            factor = factor - mul(f, factor)
+        first_t = first_t - mul_t(first_t, f)
+        if step < len(STRETCH):
+            w = mul(f, near)
+            y = near * upper_ref[...] - w.astype(BF16)
+            error = (error - near.astype(F32)) - (w + mul_t(y, f))
+            stretch = STRETCH[step]
+            error = error * stretch + jnp.where(rows == cols, stretch - 1.0, 0.0)
+    left = jnp.sum(error * error, axis=0, keepdims=True)
     x = jnp.sqrt(var_row) * dr
     diagonal = jnp.sum(jnp.where(rows == cols, factor, 0.0), axis=0, keepdims=True) * x
     scale = 1.0 / (1.0 + diagonal)
-    b = jnp.where(rows > cols, factor * (x * scale), 0.0)
-    b2 = mul(b, b)
+    b = jnp.where(rows > cols, factor * (x * scale), 0.0).astype(BF16)
+    b2 = mul(b, b).astype(BF16)
     second_t = first_t * scale
     second_t = second_t - mul(second_t, b)
+    second_t = second_t + mul(second_t, b2)
     b4 = mul(b2, b2)
-    second_t = second_t + mul(second_t, b2)
-    second_t = second_t + mul(second_t, b4)
-    left = jnp.maximum(left, jnp.sum(b4 * b4))
-    product = mul_t(first_t, second_t)
-    transform = jnp.where(rows == cols, 1.0, 0.0) - product
-    return transform.astype(BF16), left
+    left = left + B_WEIGHT * jnp.sum(b4 * b4, axis=0, keepdims=True)
+    second_t = second_t.astype(BF16)
+    first_t = first_t.astype(BF16)
+    one = jnp.where(rows == cols, 1.0, 0.0)
+    turned = (one - mul_t(second_t, first_t)).astype(BF16)
+    transform = (one - mul_t(first_t, second_t)).astype(BF16)
+    return transform, turned, left
 
 
 def exact(a, b, dims):
@@ -112,7 +121,7 @@
 
 def transform_kernel(
     near_ref, far_ref, place_ref, var_ref, var_col_ref, weights_ref,
-    obs_ref, obs_t_ref, cov_ref, inv_ref, shift_ref, *, inverse_count
+    obs_ref, obs_t_ref, lower_ref, upper_ref, cov_ref, inv_ref, shift_ref, *, inverse_count
 ):
     batches, observations = var_ref.shape
     pieces, rows_held, members = near_ref.shape
@@ -131,25 +140,25 @@
             obs_t_ref[batch] = obs_t
             obs_ref[batch] = mul_t(eye, obs_t).astype(BF16)
 
-    def advance(weights, batch):
+    def advance(weights, turned, batch):
         weights_ref[batch] = weights
         for later in range(batch + 1, batches):
-            obs = obs_ref[later]
-            obs_t = obs_t_ref[later]
-            obs_ref[later] = mul(weights, obs).astype(BF16)
-            obs_t_ref[later] = mul_t(obs_t, weights).astype(BF16)
+            obs_t_ref[later] = mul(obs_t_ref[later], turned).astype(BF16)
+            obs_ref[later] = mul(weights, obs_ref[later]).astype(BF16)
 
     load()
-    left = jnp.float32(0.0)
+    lower_ref[...] = jnp.where(rows > cols, 1.0, jnp.where(rows == cols, 0.5, 0.0)).astype(BF16)
+    upper_ref[...] = jnp.where(rows < cols, 1.0, jnp.where(rows == cols, 0.5, 0.0)).astype(BF16)
+    left = jnp.zeros((1, observations), F32)
     for batch in range(batches):
-        weights, part = fast_transform(
+        weights, turned, part = fast_transform(
             obs_ref[batch], obs_t_ref[batch], var_ref[batch : batch + 1, :],
-            var_col_ref[:, batch : batch + 1], inverse_count,
+            var_col_ref[:, batch : batch + 1], lower_ref, upper_ref, inverse_count,
         )
-        left = jnp.maximum(left, part)
-        advance(weights, batch)
-
-    @pl.when(jnp.logical_not(left <= RESIDUAL_MAX))
+        left = left + part
+        advance(weights, turned, batch)
+
+    @pl.when(jnp.logical_not(jnp.sum(left) <= RESIDUAL_MAX))
     def _():
         load()
         for batch in range(batches):
@@ -157,10 +166,10 @@
                 obs_ref[batch], obs_t_ref[batch], var_ref[batch : batch + 1, :],
                 cov_ref, inv_ref, shift_ref, inverse_count,
             )
-            advance(weights, batch)
-
-
-def transforms(near, far, place, var, members):
+            advance(weights, mul_t(eye, weights).astype(BF16), batch)
+
+
+def transforms(near, far, place, var, var_col, members):
     batches, observations = var.shape
     square = (observations, observations)
     return pl.pallas_call(
@@ -173,14 +182,16 @@
         scratch_shapes=[
             pltpu.VMEM((batches, members, observations), BF16),
             pltpu.VMEM((batches, observations, members), BF16),
+            pltpu.VMEM(square, BF16),
+            pltpu.VMEM(square, BF16),
             pltpu.VMEM(square, F32),
             pltpu.VMEM(square, F32),
             pltpu.VMEM(square, F32),
         ],
         compiler_params=pltpu.CompilerParams(vmem_limit_bytes=32 << 20),
-        cost_estimate=pl.CostEstimate(flops=8 * 10**9, bytes_accessed=1 << 20, transcendentals=0),
+        cost_estimate=pl.CostEstimate(flops=1 << 20, bytes_accessed=1 << 10, transcendentals=0),
         name="transforms",
-    )(near, far, place.T, var, var.T)
+    )(near, far, place, var, var_col)
 
 
 def apply_kernel(weights_ref, block_ref, out_ref):
@@ -206,19 +217,31 @@
     )(weights, block)
 
 
-def select_kernel(first_ref, block_ref, index_ref, seen_ref, *, block_cols):
+def select_kernel(
+    first_ref, block_ref, index_ref, seen_ref, held_ref, places_ref, sems, *, block_cols
+):
     batches = index_ref.shape[0]
     members, group_cols = block_ref.shape
     blocks = group_cols // block_cols
-    local = index_ref[...] - first_ref[0]
+    ranges = [slice(k * block_cols, (k + 1) * block_cols) for k in range(blocks)]
+    copies = [pltpu.make_async_copy(index_ref, places_ref, sems.at[blocks])]
+    for block, part in enumerate(ranges):
+        copies.append(
+            pltpu.make_async_copy(block_ref.at[:, part], held_ref.at[:, part], sems.at[block])
+        )
+    for copy in copies:
+        copy.start()
+    copies[0].wait()
+    local = places_ref[...] - first_ref[0]
     lane = lax.broadcasted_iota(jnp.int32, (1, block_cols), 1)
     slot = lax.broadcasted_iota(jnp.int32, (1, PAD), 1)
     seen = jnp.zeros((members, PAD), F32)
-    for block in range(blocks):
+    for block, part in enumerate(ranges):
         inside = local - block * block_cols
         inside = jnp.where((inside >= 0) & (inside < block_cols), inside, 0).astype(F32)
         offsets = jnp.sum(inside, axis=1, keepdims=True).astype(jnp.int32)
-        values = block_ref[:, block * block_cols : (block + 1) * block_cols].astype(F32)
+        copies[block + 1].wait()
+        values = held_ref[:, part].astype(F32)
         for batch in range(batches):
             chosen = jnp.where(lane == offsets[batch : batch + 1, :], values, 0.0)
             column = jnp.sum(chosen, axis=1, keepdims=True)
@@ -229,14 +252,19 @@
 
 
 def select(perturbations, index, first, block_cols, peers):
-    members = perturbations.shape[0]
+    members, group_cols = perturbations.shape
     return pl.pallas_call(
         lambda *refs: select_kernel(*refs, block_cols=block_cols),
         out_shape=jax.ShapeDtypeStruct((peers, members, PAD), BF16),
         in_specs=[pl.BlockSpec(memory_space=pltpu.SMEM)]
-        + [pl.BlockSpec(memory_space=pltpu.VMEM)] * 2,
+        + [pl.BlockSpec(memory_space=pltpu.HBM)] * 2,
         out_specs=pl.BlockSpec(memory_space=pltpu.VMEM),
-        compiler_params=pltpu.CompilerParams(vmem_limit_bytes=16 << 20),
+        scratch_shapes=[
+            pltpu.VMEM(perturbations.shape, BF16),
+            pltpu.VMEM(index.shape, jnp.int32),
+            pltpu.SemaphoreType.DMA((group_cols // block_cols + 1,)),
+        ],
+        compiler_params=pltpu.CompilerParams(vmem_limit_bytes=60 << 20),
         name="select",
     )(first.reshape(1), perturbations, index)
 
@@ -266,15 +294,17 @@
     sent = select(perturbations, obs_index, first, block_cols, mem_count)
     seen_group = lax.all_to_all(sent, "mem", split_axis=0, concat_axis=0, tiled=True)
     arranged = perturbations.reshape(members_here, mem_count, block_cols).transpose(1, 0, 2)
-    arranged, seen_group = lax.optimization_barrier((arranged, seen_group))
+    away = (obs_index // group_cols) ^ lax.axis_index("col").astype(jnp.int32)
+    piece = sum(jnp.where(away == p, at, 0) for at, p in enumerate(PIECES))
+    place = (piece * mem_count + obs_index % group_cols // block_cols).T
+    arranged, seen_group, place, var_row, var_col = lax.optimization_barrier(
+        (arranged, seen_group, place, obs_var, obs_var.T)
+    )
     block = lax.all_to_all(arranged, "mem", split_axis=0, concat_axis=0, tiled=True)
     block = block.reshape(members, block_cols)
     seen_group = seen_group.reshape(members, PAD)[:, :owned].T
     near, far = gather_col(seen_group[None], col_count)
-    away = (obs_index // group_cols) ^ lax.axis_index("col").astype(jnp.int32)
-    piece = sum(jnp.where(away == p, at, 0) for at, p in enumerate(PIECES))
-    place = piece * mem_count + obs_index % group_cols // block_cols
-    weights = transforms(near, far, place, obs_var, members)
+    weights = transforms(near, far, place, var_row, var_col, members)
     ensemble = apply(weights, block)
     returned = lax.all_to_all(
         ensemble.reshape(mem_count, members_here, block_cols), "mem",

time: 286 us -> 286 us (level)
    ppermute x5, waiting for transfers between devices: 2.38 us -> 6.57 us  [swapped(): return lax.ppermute(value, 'col', [(i, i ^ bits) for i in range(count)])]
  transfers between devices with their start and end apart: 7 -> 7, of which waited for: 3 -> 4; matrix products, arithmetic and copies ran while one was open for 1% -> 1% of each run, Pallas kernels for 77% -> 76%
where the time goes in v3:
time: 286 us; the launch traced here: 285 us
  Pallas kernels  221 us (77%)
  blocking collectives  25.4 us (9%)
  starting transfers between devices  21 us (7%)
  waiting for transfers between devices  13.4 us (5%)
    pallas_call x1, Pallas kernels, transforms(): pl.pallas_call(lambda *refs: transform_kernel(*refs, inverse_count=1.0 /...  217 us
    all_to_all x1, blocking collectives, on_device(): lax.all_to_all(ensemble.reshape(mem_count, members_here, block_cols), 'me...  25.4 us
    all_to_all x1, starting transfers between devices, on_device(): lax.all_to_all(sent, 'mem', split_axis=0, concat_axis=0, tiled=True)  9.59 us
    ppermute x5, starting transfers between devices, swapped(): return lax.ppermute(value, 'col', [(i, i ^ bits) for i in range(count)])  7.87 us
    all_to_all x1, waiting for transfers between devices, on_device(): lax.all_to_all(sent, 'mem', split_axis=0, concat_axis=0, tiled=True)  6.81 us
    ppermute x5, waiting for transfers between devices, swapped(): return lax.ppermute(value, 'col', [(i, i ^ bits) for i in range(count)])  6.57 us
  transfers between devices with their start and end apart: 7, of which 4 were waited for; matrix products, arithmetic and copies ran while one was open for 1% of the time, Pallas kernels for 76%

profile of v3, /device:TPU:2, one launch (start us, length us, event | category | flops | bytes accessed | tf_op | source)
XLA Modules:
  0.0 284.5 jit_solution(8250936907043455912)
XLA Ops:
  0.0 0.0 copy-start.1
  0.0 3.4 %select.11 = bf16[16,16,128]{2,1,0:T(8,128)(2,1)} custom-call(s32[1]{0:T(128)} %bitcast.1.refs_0_, bf16[16,16384]{1,0:T(8,128)(2,1)} %refs_1_.1, s32[4,256]{1,0:T(4,128)} %refs_2_.1), custom_call_target="tpu_custom_call" | custom-call | tf_op jit(solution)/shard_map/select/pallas_call | solution.py:256
  3.4 0.0 copy-start.2
  3.4 9.6 %all-to-all-start = ((bf16[16,16,128]{2,1,0:T(8,128)(2,1)}), bf16[16,16,128]{2,1,0:T(8,128)(2,1)S(1)}, u32[]{:S(2)}, u32[]{:S(2)}) async-start(bf16[16,16,128]{2,1,0:T(8,128)(2,1)} %select.11), calls=%async_computation | async-start | bytes 131072 | tf_op jit(solution)/shard_map/all_to_all | solution.py:295
  13.0 0.0 copy-done.2
  13.0 0.1 copy.16
  13.2 0.0 copy-start
  13.2 0.2 copy.21
  13.4 0.5 copy-done
  13.9 0.1 copy.23
  14.0 0.0 copy-done.1
  14.0 0.8 copy.30
  14.8 0.4 fusion.3.refs_2_
  15.2 6.8 %all-to-all-done = bf16[16,16,128]{2,1,0:T(8,128)(2,1)S(1)} async-done(((bf16[16,16,128]{2,1,0:T(8,128)(2,1)}), bf16[16,16,128]{2,1,0:T(8,128)(2,1)S(1)}, u32[]{:S(2)}, u32[]{:S(2)}) %all-to-all-start) | async-done | bytes 65568 | tf_op jit(solution)/shard_map/all_to_all | solution.py:295
  22.0 0.1 copy.26
  22.1 3.6 %all-to-all-start.1 = ((bf16[16,16,1024]{2,1,0:T(8,128)(2,1)}), bf16[16,16,1024]{2,1,0:T(8,128)(2,1)S(1)}, u32[]{:S(2)}, u32[]{:S(2)}) async-start(bf16[16,16,1024]{2,1,0:T(8,128)(2,1)} %bitcast.20), calls=%async_computation.1 | async-start | bytes 1048576 | tf_op jit(solution)/shard_map/all_to_all | solution.py:303
  25.7 3.0 %collective-permute-start = (bf16[1,64,256]{2,1,0:T(8,128)(2,1)S(1)}, bf16[1,64,256]{2,1,0:T(8,128)(2,1)S(1)}, u32[]{:S(2)}, u32[]{:S(2)}) collective-permute-start(bf16[1,64,256]{2,1,0:T(8,128)(2,1)S(1)} %bitcast.27), channel_id=1, source_target_pairs={{0,8},{1,9},{2,10},{3,11},{4,12},{5,13},{6,14},{7,15},{8,0},{9,1},... | collective-permute-start | bytes 98312 | tf_op jit(solution)/shard_map/ppermute | solution.py:273
  28.7 2.8 collective-permute-done
  31.5 2.2 collective-permute-start.3
  33.7 0.0 collective-permute-start.2
  33.8 2.6 collective-permute-start.1
  36.3 2.2 collective-permute-done.1
  38.6 0.0 collective-permute-done.2
  38.6 0.0 collective-permute-done.3
  38.6 0.1 collective-permute-start.4
  38.7 1.5 collective-permute-done.4.refs_1_
  40.2 216.5 %transforms.1.weights_ref = bf16[4,256,256]{2,1,0:T(8,128)(2,1)S(1)} custom-call(bf16[8,64,256]{2,1,0:T(8,128)(2,1)S(1)} %constant_dynamic-update-slice_fusion.refs_0_, bf16[8,64,256]{2,1,0:T(8,128)(2,1)S(1)} %collective-permute-done.4.refs_1_, s32[256,4]{1,0:T(8,128)S(1)} %fusion.3.refs_2_, f32[4,256]{1,0:T(4,128)S(1)} %copy-done, f32[256,4]{1,0:T(8,128)S(1)} %bitcast.24), custom_call_target="tpu_custom_call" | custom-call | flops 1048576 | bytes 1024 | tf_op jit(solution)/shard_map/transforms/pallas_call | solution.py:175
  256.8 0.0 all-to-all-done.1
  256.8 1.5 apply.1
  258.3 25.4 %all_to_all.15 = bf16[16,16,1024]{2,1,0:T(8,128)(2,1)S(1)} all-to-all(bf16[16,16,1024]{2,1,0:T(8,128)(2,1)S(1)} %bitcast.23), channel_id=1, replica_groups=mesh['mem'=16,'col'=16] {'mem'}, dimensions={0} | all-to-all | bytes 1048576 | tf_op jit(solution)/shard_map/all_to_all | solution.py:309
  283.7 0.8 copy.28
  (7 shorter events, 0.0 us)
Async XLA Ops:
  0.0 14.0 %copy-start.1 = (bf16[16,16384]{1,0:T(8,128)(2,1)S(1)}, bf16[16,16384]{1,0:T(8,128)(2,1)}, u32[]{:S(2)}) copy-start(bf16[16,16384]{1,0:T(8,128)(2,1)} %refs_1_.1) | copy-start | bytes 1572868
  3.4 9.6 %copy-start.2 = (s32[4,256]{1,0:T(4,128)S(1)}, s32[4,256]{1,0:T(4,128)}, u32[]{:S(2)}) copy-start(s32[4,256]{1,0:T(4,128)} %refs_2_.1) | copy-start | bytes 12292
  3.4 18.6 %all-to-all-start = ((bf16[16,16,128]{2,1,0:T(8,128)(2,1)}), bf16[16,16,128]{2,1,0:T(8,128)(2,1)S(1)}, u32[]{:S(2)}, u32[]{:S(2)}) async-start(bf16[16,16,128]{2,1,0:T(8,128)(2,1)} %select.11), calls=%async_computation | async-start | bytes 131072 | tf_op jit(solution)/shard_map/all_to_all | solution.py:295
  13.2 0.7 copy-start
  22.1 234.6 %all-to-all-start.1 = ((bf16[16,16,1024]{2,1,0:T(8,128)(2,1)}), bf16[16,16,1024]{2,1,0:T(8,128)(2,1)S(1)}, u32[]{:S(2)}, u32[]{:S(2)}) async-start(bf16[16,16,1024]{2,1,0:T(8,128)(2,1)} %bitcast.20), calls=%async_computation.1 | async-start | bytes 1048576 | tf_op jit(solution)/shard_map/all_to_all | solution.py:303
  25.7 5.8 %collective-permute-start = (bf16[1,64,256]{2,1,0:T(8,128)(2,1)S(1)}, bf16[1,64,256]{2,1,0:T(8,128)(2,1)S(1)}, u32[]{:S(2)}, u32[]{:S(2)}) collective-permute-start(bf16[1,64,256]{2,1,0:T(8,128)(2,1)S(1)} %bitcast.27), channel_id=1, source_target_pairs={{0,8},{1,9},{2,10},{3,11},{4,12},{5,13},{6,14},{7,15},{8,0},{9,1},... | collective-permute-start | bytes 98312 | tf_op jit(solution)/shard_map/ppermute | solution.py:273
  31.5 7.1 %collective-permute-start.3 = (bf16[2,64,256]{2,1,0:T(8,128)(2,1)S(1)}, bf16[2,64,256]{2,1,0:T(8,128)(2,1)S(1)}, u32[]{:S(2)}, u32[]{:S(2)}) collective-permute-start(bf16[2,64,256]{2,1,0:T(8,128)(2,1)S(1)} %pad_maximum_fusion), channel_id=1, source_target_pairs={{0,4},{1,5},{2,6},{3,7},{4,0},{5,1},{6,2},{7,3},{8,12},{9,13},{10,... | collective-permute-start | bytes 196616 | tf_op jit(solution)/shard_map/ppermute | solution.py:273
  33.7 4.8 %collective-permute-start.2 = (bf16[2,64,256]{2,1,0:T(8,128)(2,1)S(1)}, bf16[2,64,256]{2,1,0:T(8,128)(2,1)S(1)}, u32[]{:S(2)}, u32[]{:S(2)}) collective-permute-start(bf16[2,64,256]{2,1,0:T(8,128)(2,1)S(1)} %pad_maximum_fusion), channel_id=1, source_target_pairs={{0,6},{1,7},{2,4},{3,5},{4,2},{5,3},{6,0},{7,1},{8,14},{9,15},{10,... | collective-permute-start | bytes 196616 | tf_op jit(solution)/shard_map/ppermute | solution.py:273
  33.8 4.8 %collective-permute-start.1 = (bf16[2,64,256]{2,1,0:T(8,128)(2,1)S(1)}, bf16[2,64,256]{2,1,0:T(8,128)(2,1)S(1)}, u32[]{:S(2)}, u32[]{:S(2)}) collective-permute-start(bf16[2,64,256]{2,1,0:T(8,128)(2,1)S(1)} %pad_maximum_fusion), channel_id=1, source_target_pairs={{0,2},{1,3},{2,0},{3,1},{4,6},{5,7},{6,4},{7,5},{8,10},{9,11},{10,... | collective-permute-start | bytes 196616 | tf_op jit(solution)/shard_map/ppermute | solution.py:273
  38.6 1.6 collective-permute-start.4

commit v4 on v3

--- a/solution.py
+++ b/solution.py
@@ -189,7 +189,7 @@
             pltpu.VMEM(square, F32),
         ],
         compiler_params=pltpu.CompilerParams(vmem_limit_bytes=32 << 20),
-        cost_estimate=pl.CostEstimate(flops=1 << 20, bytes_accessed=1 << 10, transcendentals=0),
+        cost_estimate=pl.CostEstimate(flops=3 * 10**9, bytes_accessed=1 << 10, transcendentals=0),
         name="transforms",
     )(near, far, place, var, var_col)
 
@@ -224,26 +224,25 @@
     members, group_cols = block_ref.shape
     blocks = group_cols // block_cols
     ranges = [slice(k * block_cols, (k + 1) * block_cols) for k in range(blocks)]
-    copies = [pltpu.make_async_copy(index_ref, places_ref, sems.at[blocks])]
-    for block, part in enumerate(ranges):
-        copies.append(
-            pltpu.make_async_copy(block_ref.at[:, part], held_ref.at[:, part], sems.at[block])
-        )
-    for copy in copies:
-        copy.start()
-    copies[0].wait()
+    fetch_places = pltpu.make_async_copy(index_ref, places_ref, sems.at[0])
+    fetch_block = pltpu.make_async_copy(block_ref, held_ref, sems.at[1])
+    fetch_places.start()
+    fetch_block.start()
+    fetch_places.wait()
     local = places_ref[...] - first_ref[0]
     lane = lax.broadcasted_iota(jnp.int32, (1, block_cols), 1)
     slot = lax.broadcasted_iota(jnp.int32, (1, PAD), 1)
+    offsets = []
+    for block in range(blocks):
+        inside = local - block * block_cols
+        inside = jnp.where((inside >= 0) & (inside < block_cols), inside, 0).astype(F32)
+        offsets.append(jnp.sum(inside, axis=1, keepdims=True).astype(jnp.int32))
+    fetch_block.wait()
     seen = jnp.zeros((members, PAD), F32)
     for block, part in enumerate(ranges):
-        inside = local - block * block_cols
-        inside = jnp.where((inside >= 0) & (inside < block_cols), inside, 0).astype(F32)
-        offsets = jnp.sum(inside, axis=1, keepdims=True).astype(jnp.int32)
-        copies[block + 1].wait()
         values = held_ref[:, part].astype(F32)
         for batch in range(batches):
-            chosen = jnp.where(lane == offsets[batch : batch + 1, :], values, 0.0)
+            chosen = jnp.where(lane == offsets[block][batch : batch + 1, :], values, 0.0)
             column = jnp.sum(chosen, axis=1, keepdims=True)
             seen = jnp.where(slot == batch * blocks + block, column, seen)
     seen = seen.astype(BF16)
@@ -252,7 +251,7 @@
 
 
 def select(perturbations, index, first, block_cols, peers):
-    members, group_cols = perturbations.shape
+    members = perturbations.shape[0]
     return pl.pallas_call(
         lambda *refs: select_kernel(*refs, block_cols=block_cols),
         out_shape=jax.ShapeDtypeStruct((peers, members, PAD), BF16),
@@ -262,7 +261,7 @@
         scratch_shapes=[
             pltpu.VMEM(perturbations.shape, BF16),
             pltpu.VMEM(index.shape, jnp.int32),
-            pltpu.SemaphoreType.DMA((group_cols // block_cols + 1,)),
+            pltpu.SemaphoreType.DMA((2,)),
         ],
         compiler_params=pltpu.CompilerParams(vmem_limit_bytes=60 << 20),
         name="select",

time: 286 us -> 282 us (0.986)
  transfers between devices with their start and end apart: 7 -> 7, of which waited for: 4 -> 3; matrix products, arithmetic and copies ran while one was open for 1% -> 1% of each run, Pallas kernels for 76% -> 77%
where the time goes in v4:
time: 282 us; the launch traced here: 281 us
  Pallas kernels  220 us (78%)
  blocking collectives  25.8 us (9%)
  starting transfers between devices  21 us (7%)
  waiting for transfers between devices  10.6 us (4%)
    pallas_call x1, Pallas kernels, transforms(): pl.pallas_call(lambda *refs: transform_kernel(*refs, inverse_count=1.0 /...  216 us
    all_to_all x1, blocking collectives, on_device(): lax.all_to_all(ensemble.reshape(mem_count, members_here, block_cols), 'me...  25.8 us
    all_to_all x1, starting transfers between devices, on_device(): lax.all_to_all(sent, 'mem', split_axis=0, concat_axis=0, tiled=True)  9.59 us
    ppermute x5, starting transfers between devices, swapped(): return lax.ppermute(value, 'col', [(i, i ^ bits) for i in range(count)])  7.87 us
    all_to_all x1, waiting for transfers between devices, on_device(): lax.all_to_all(sent, 'mem', split_axis=0, concat_axis=0, tiled=True)  6.81 us
  transfers between devices with their start and end apart: 7, of which 3 were waited for; matrix products, arithmetic and copies ran while one was open for 1% of the time, Pallas kernels for 77%

profile of v4, /device:TPU:2, one launch (start us, length us, event | category | flops | bytes accessed | tf_op | source)
XLA Modules:
  0.0 280.9 jit_solution(11488958848503461689)
XLA Ops:
  0.0 0.0 copy-start.1
  0.0 2.3 select.11
  2.3 0.0 copy-start.2
  2.3 9.6 %all-to-all-start = ((bf16[16,16,128]{2,1,0:T(8,128)(2,1)}), bf16[16,16,128]{2,1,0:T(8,128)(2,1)S(1)}, u32[]{:S(2)}, u32[]{:S(2)}) async-start(bf16[16,16,128]{2,1,0:T(8,128)(2,1)} %select.11), calls=%async_computation | async-start | bytes 131072 | tf_op jit(solution)/shard_map/all_to_all | solution.py:294
  11.9 0.0 copy-done.2
  11.9 0.1 copy.16
  12.1 0.0 copy-start
  12.1 0.2 copy.21
  12.3 0.5 copy-done
  12.8 0.1 copy.23
  12.9 0.0 copy-done.1
  12.9 0.8 copy.30
  13.8 0.4 fusion.3.refs_2_
  14.2 6.8 %all-to-all-done = bf16[16,16,128]{2,1,0:T(8,128)(2,1)S(1)} async-done(((bf16[16,16,128]{2,1,0:T(8,128)(2,1)}), bf16[16,16,128]{2,1,0:T(8,128)(2,1)S(1)}, u32[]{:S(2)}, u32[]{:S(2)}) %all-to-all-start) | async-done | bytes 65568 | tf_op jit(solution)/shard_map/all_to_all | solution.py:294
  21.0 0.1 copy.26
  21.1 3.0 %collective-permute-start = (bf16[1,64,256]{2,1,0:T(8,128)(2,1)S(1)}, bf16[1,64,256]{2,1,0:T(8,128)(2,1)S(1)}, u32[]{:S(2)}, u32[]{:S(2)}) collective-permute-start(bf16[1,64,256]{2,1,0:T(8,128)(2,1)S(1)} %bitcast.27), channel_id=1, source_target_pairs={{0,8},{1,9},{2,10},{3,11},{4,12},{5,13},{6,14},{7,15},{8,0},{9,1},... | collective-permute-start | bytes 98312 | tf_op jit(solution)/shard_map/ppermute | solution.py:272
  24.1 3.6 %all-to-all-start.1 = ((bf16[16,16,1024]{2,1,0:T(8,128)(2,1)}), bf16[16,16,1024]{2,1,0:T(8,128)(2,1)S(1)}, u32[]{:S(2)}, u32[]{:S(2)}) async-start(bf16[16,16,1024]{2,1,0:T(8,128)(2,1)} %bitcast.20), calls=%async_computation.1 | async-start | bytes 1048576 | tf_op jit(solution)/shard_map/all_to_all | solution.py:302
  27.6 0.0 collective-permute-done
  27.7 2.2 collective-permute-start.3
  29.9 0.0 collective-permute-start.2
  29.9 2.6 collective-permute-start.1
  32.5 2.2 collective-permute-done.1
  34.7 0.0 collective-permute-done.2
  34.7 0.0 collective-permute-done.3
  34.8 0.1 collective-permute-start.4
  34.9 1.5 collective-permute-done.4.refs_1_
  36.4 216.5 %transforms.1.weights_ref = bf16[4,256,256]{2,1,0:T(8,128)(2,1)S(1)} custom-call(bf16[8,64,256]{2,1,0:T(8,128)(2,1)S(1)} %constant_dynamic-update-slice_fusion.refs_0_, bf16[8,64,256]{2,1,0:T(8,128)(2,1)S(1)} %collective-permute-done.4.refs_1_, s32[256,4]{1,0:T(8,128)S(1)} %fusion.3.refs_2_, f32[4,256]{1,0:T(4,128)S(1)} %copy-done, f32[256,4]{1,0:T(8,128)S(1)} %bitcast.24), custom_call_target="tpu_custom_call" | custom-call | flops 3000000000 | bytes 1024 | tf_op jit(solution)/shard_map/transforms/pallas_call | solution.py:175
  252.8 0.0 all-to-all-done.1
  252.9 1.5 apply.1
  254.4 25.8 %all_to_all.15 = bf16[16,16,1024]{2,1,0:T(8,128)(2,1)S(1)} all-to-all(bf16[16,16,1024]{2,1,0:T(8,128)(2,1)S(1)} %bitcast.23), channel_id=1, replica_groups=mesh['mem'=16,'col'=16] {'mem'}, dimensions={0} | all-to-all | bytes 1048576 | tf_op jit(solution)/shard_map/all_to_all | solution.py:308
  280.1 0.8 copy.28
  (7 shorter events, 0.0 us)
Async XLA Ops:
  0.0 12.9 %copy-start.1 = (bf16[16,16384]{1,0:T(8,128)(2,1)S(1)}, bf16[16,16384]{1,0:T(8,128)(2,1)}, u32[]{:S(2)}) copy-start(bf16[16,16384]{1,0:T(8,128)(2,1)} %refs_1_.1) | copy-start | bytes 1572868
  2.3 9.6 %copy-start.2 = (s32[4,256]{1,0:T(4,128)S(1)}, s32[4,256]{1,0:T(4,128)}, u32[]{:S(2)}) copy-start(s32[4,256]{1,0:T(4,128)} %refs_2_.1) | copy-start | bytes 12292
  2.3 18.6 %all-to-all-start = ((bf16[16,16,128]{2,1,0:T(8,128)(2,1)}), bf16[16,16,128]{2,1,0:T(8,128)(2,1)S(1)}, u32[]{:S(2)}, u32[]{:S(2)}) async-start(bf16[16,16,128]{2,1,0:T(8,128)(2,1)} %select.11), calls=%async_computation | async-start | bytes 131072 | tf_op jit(solution)/shard_map/all_to_all | solution.py:294
  12.1 0.7 copy-start
  21.1 6.6 %collective-permute-start = (bf16[1,64,256]{2,1,0:T(8,128)(2,1)S(1)}, bf16[1,64,256]{2,1,0:T(8,128)(2,1)S(1)}, u32[]{:S(2)}, u32[]{:S(2)}) collective-permute-start(bf16[1,64,256]{2,1,0:T(8,128)(2,1)S(1)} %bitcast.27), channel_id=1, source_target_pairs={{0,8},{1,9},{2,10},{3,11},{4,12},{5,13},{6,14},{7,15},{8,0},{9,1},... | collective-permute-start | bytes 98312 | tf_op jit(solution)/shard_map/ppermute | solution.py:272
  24.1 228.8 %all-to-all-start.1 = ((bf16[16,16,1024]{2,1,0:T(8,128)(2,1)}), bf16[16,16,1024]{2,1,0:T(8,128)(2,1)S(1)}, u32[]{:S(2)}, u32[]{:S(2)}) async-start(bf16[16,16,1024]{2,1,0:T(8,128)(2,1)} %bitcast.20), calls=%async_computation.1 | async-start | bytes 1048576 | tf_op jit(solution)/shard_map/all_to_all | solution.py:302
  27.7 7.1 %collective-permute-start.3 = (bf16[2,64,256]{2,1,0:T(8,128)(2,1)S(1)}, bf16[2,64,256]{2,1,0:T(8,128)(2,1)S(1)}, u32[]{:S(2)}, u32[]{:S(2)}) collective-permute-start(bf16[2,64,256]{2,1,0:T(8,128)(2,1)S(1)} %pad_maximum_fusion), channel_id=1, source_target_pairs={{0,4},{1,5},{2,6},{3,7},{4,0},{5,1},{6,2},{7,3},{8,12},{9,13},{10,... | collective-permute-start | bytes 196616 | tf_op jit(solution)/shard_map/ppermute | solution.py:272
  29.9 4.8 %collective-permute-start.2 = (bf16[2,64,256]{2,1,0:T(8,128)(2,1)S(1)}, bf16[2,64,256]{2,1,0:T(8,128)(2,1)S(1)}, u32[]{:S(2)}, u32[]{:S(2)}) collective-permute-start(bf16[2,64,256]{2,1,0:T(8,128)(2,1)S(1)} %pad_maximum_fusion), channel_id=1, source_target_pairs={{0,6},{1,7},{2,4},{3,5},{4,2},{5,3},{6,0},{7,1},{8,14},{9,15},{10,... | collective-permute-start | bytes 196616 | tf_op jit(solution)/shard_map/ppermute | solution.py:272
  29.9 4.8 %collective-permute-start.1 = (bf16[2,64,256]{2,1,0:T(8,128)(2,1)S(1)}, bf16[2,64,256]{2,1,0:T(8,128)(2,1)S(1)}, u32[]{:S(2)}, u32[]{:S(2)}) collective-permute-start(bf16[2,64,256]{2,1,0:T(8,128)(2,1)S(1)} %pad_maximum_fusion), channel_id=1, source_target_pairs={{0,2},{1,3},{2,0},{3,1},{4,6},{5,7},{6,4},{7,5},{8,10},{9,11},{10,... | collective-permute-start | bytes 196616 | tf_op jit(solution)/shard_map/ppermute | solution.py:272
  34.8 1.6 collective-permute-start.4

commit v5 on v4

--- a/solution.py
+++ b/solution.py
@@ -120,13 +120,13 @@
 
 
 def transform_kernel(
-    near_ref, far_ref, place_ref, var_ref, var_col_ref, weights_ref,
-    obs_ref, obs_t_ref, lower_ref, upper_ref, cov_ref, inv_ref, shift_ref, *, inverse_count
+    *refs, inverse_count
 ):
+    (*part_refs, place_ref, var_ref, var_col_ref, weights_ref,
+     obs_ref, obs_t_ref, lower_ref, upper_ref, cov_ref, inv_ref, shift_ref) = refs
     batches, observations = var_ref.shape
-    pieces, rows_held, members = near_ref.shape
+    pieces, rows_held, members = part_refs[0].shape
     per_batch = rows_held // batches
-    half = pieces * per_batch
     rows, cols = iotas(observations)
     eye = jnp.where(rows == cols, 1.0, 0.0).astype(BF16)
 
@@ -134,9 +134,8 @@
         for batch in range(batches):
             order = jnp.where(cols == place_ref[:, batch : batch + 1], 1.0, 0.0)
             held = slice(batch * per_batch, (batch + 1) * per_batch)
-            near = near_ref[:, held, :].reshape(half, members)
-            far = far_ref[:, held, :].reshape(half, members)
-            obs_t = mul(order, jnp.concatenate([near, far])).astype(BF16)
+            parts = [ref[:, held, :].reshape(pieces * per_batch, members) for ref in part_refs]
+            obs_t = mul(order, jnp.concatenate(parts)).astype(BF16)
             obs_t_ref[batch] = obs_t
             obs_ref[batch] = mul_t(eye, obs_t).astype(BF16)
 
@@ -169,7 +168,7 @@
             advance(weights, mul_t(eye, weights).astype(BF16), batch)
 
 
-def transforms(near, far, place, var, var_col, members):
+def transforms(parts, place, var, var_col, members):
     batches, observations = var.shape
     square = (observations, observations)
     return pl.pallas_call(
@@ -177,7 +176,7 @@
             *refs, inverse_count=1.0 / (members - 1)
         ),
         out_shape=jax.ShapeDtypeStruct((batches, members, members), BF16),
-        in_specs=[pl.BlockSpec(memory_space=pltpu.VMEM)] * 5,
+        in_specs=[pl.BlockSpec(memory_space=pltpu.VMEM)] * (len(parts) + 3),
         out_specs=pl.BlockSpec(memory_space=pltpu.VMEM),
         scratch_shapes=[
             pltpu.VMEM((batches, members, observations), BF16),
@@ -189,9 +188,9 @@
             pltpu.VMEM(square, F32),
         ],
         compiler_params=pltpu.CompilerParams(vmem_limit_bytes=32 << 20),
-        cost_estimate=pl.CostEstimate(flops=3 * 10**9, bytes_accessed=1 << 10, transcendentals=0),
+        cost_estimate=pl.CostEstimate(flops=8 * 10**9, bytes_accessed=1 << 10, transcendentals=0),
         name="transforms",
-    )(near, far, place, var, var_col)
+    )(*parts, place, var, var_col)
 
 
 def apply_kernel(weights_ref, block_ref, out_ref):
@@ -274,11 +273,18 @@
 
 def gather_col(own, count):
     pair = jnp.concatenate([own, swapped(own, 8, count)])
-    half = jnp.concatenate([pair] + [swapped(pair, bits, count) for bits in (2, 6, 4)])
-    return half, swapped(half, 1, count)
-
-
-PIECES = [p ^ q ^ r for r in (0, 1) for q in (0, 2, 6, 4) for p in (0, 8)]
+    return [pair] + [swapped(pair, bits, count) for bits in (2, 6, 4)]
+
+
+PIECES = [q ^ p for q in (0, 2, 6, 4) for p in (0, 8)]
+CORES = 2
+
+
+def chip_groups(mem_count, col_count):
+    return [
+        [mem * col_count + first + core for core in range(CORES) for mem in range(mem_count)]
+        for first in range(0, col_count, CORES)
+    ]
 
 
 def on_device(perturbations, obs_index, obs_var):
@@ -290,20 +296,24 @@
     batches = obs_index.shape[0]
     owned = batches * mem_count
     first = lax.axis_index("col").astype(jnp.int32) * group_cols
-    sent = select(perturbations, obs_index, first, block_cols, mem_count)
-    seen_group = lax.all_to_all(sent, "mem", split_axis=0, concat_axis=0, tiled=True)
+    sent = select(perturbations, obs_index, first, block_cols, CORES * mem_count)
+    seen_group = lax.all_to_all(
+        sent, ("mem", "col"), split_axis=0, concat_axis=0, tiled=True,
+        axis_index_groups=chip_groups(mem_count, col_count),
+    )
     arranged = perturbations.reshape(members_here, mem_count, block_cols).transpose(1, 0, 2)
-    away = (obs_index // group_cols) ^ lax.axis_index("col").astype(jnp.int32)
-    piece = sum(jnp.where(away == p, at, 0) for at, p in enumerate(PIECES))
+    owner = obs_index // group_cols
+    away = (owner ^ lax.axis_index("col").astype(jnp.int32)) // CORES * CORES
+    piece = sum(jnp.where(away == p, at * CORES, 0) for at, p in enumerate(PIECES)) + owner % CORES
     place = (piece * mem_count + obs_index % group_cols // block_cols).T
     arranged, seen_group, place, var_row, var_col = lax.optimization_barrier(
         (arranged, seen_group, place, obs_var, obs_var.T)
     )
     block = lax.all_to_all(arranged, "mem", split_axis=0, concat_axis=0, tiled=True)
     block = block.reshape(members, block_cols)
-    seen_group = seen_group.reshape(members, PAD)[:, :owned].T
-    near, far = gather_col(seen_group[None], col_count)
-    weights = transforms(near, far, place, var_row, var_col, members)
+    seen_group = seen_group.reshape(CORES, members, PAD)[:, :, :owned].transpose(0, 2, 1)
+    parts = gather_col(seen_group, col_count)
+    weights = transforms(parts, place, var_row, var_col, members)
     ensemble = apply(weights, block)
     returned = lax.all_to_all(
         ensemble.reshape(mem_count, members_here, block_cols), "mem",

time: 282 us -> 282 us (level)
    ppermute x5 -> x4, starting transfers between devices: 7.87 us -> 7.77 us  [swapped(): return lax.ppermute(value, 'col', [(i, i ^ bits) for i in range(count)])]
  transfers between devices with their start and end apart: 7 -> 6, of which waited for: 3 -> 4; matrix products, arithmetic and copies ran while one was open for 1% -> 1% of each run, Pallas kernels for 77% -> 77%
where the time goes in v5:
time: 282 us; the launch traced here: 281 us
  Pallas kernels  220 us (78%)
  blocking collectives  24.4 us (9%)
  starting transfers between devices  21.2 us (8%)
  waiting for transfers between devices  12.2 us (4%)
    pallas_call x1, Pallas kernels, transforms(): pl.pallas_call(lambda *refs: transform_kernel(*refs, inverse_count=1.0 /...  216 us
    all_to_all x1, blocking collectives, on_device(): lax.all_to_all(ensemble.reshape(mem_count, members_here, block_cols), 'me...  24.4 us
    all_to_all x1, starting transfers between devices, on_device(): lax.all_to_all(sent, ('mem', 'col'), split_axis=0, concat_axis=0, tiled=T...  9.88 us
    ppermute x4, starting transfers between devices, swapped(): return lax.ppermute(value, 'col', [(i, i ^ bits) for i in range(count)])  7.77 us
    all_to_all x1, waiting for transfers between devices, on_device(): lax.all_to_all(sent, ('mem', 'col'), split_axis=0, concat_axis=0, tiled=T...  7.5 us
  transfers between devices with their start and end apart: 6, of which 4 were waited for; matrix products, arithmetic and copies ran while one was open for 1% of the time, Pallas kernels for 77%

profile of v5, /device:TPU:2, one launch (start us, length us, event | category | flops | bytes accessed | tf_op | source)
XLA Modules:
  0.0 281.4 jit_solution(7498667251689963441)
XLA Ops:
  0.0 0.0 copy-start.1
  0.0 2.3 select.17
  2.3 0.0 copy-start.2
  2.4 9.9 %all-to-all-start = ((bf16[32,16,128]{2,1,0:T(8,128)(2,1)}), bf16[32,16,128]{2,1,0:T(8,128)(2,1)S(1)}, u32[]{:S(2)}, u32[]{:S(2)}) async-start(bf16[32,16,128]{2,1,0:T(8,128)(2,1)} %select.17), calls=%async_computation | async-start | bytes 262144 | tf_op jit(solution)/shard_map/all_to_all | solution.py:300
  12.2 0.0 copy-done.2
  12.3 0.1 copy.15
  12.4 0.0 copy-start
  12.4 0.2 copy.20
  12.6 0.5 copy-done
  13.1 0.1 copy.22
  13.2 0.0 copy-done.1
  13.3 0.8 copy.29
  14.1 0.4 fusion.6.refs_4_
  14.5 7.5 %all-to-all-done = bf16[32,16,128]{2,1,0:T(8,128)(2,1)S(1)} async-done(((bf16[32,16,128]{2,1,0:T(8,128)(2,1)}), bf16[32,16,128]{2,1,0:T(8,128)(2,1)S(1)}, u32[]{:S(2)}, u32[]{:S(2)}) %all-to-all-start) | async-done | bytes 131104 | tf_op jit(solution)/shard_map/all_to_all | solution.py:300
  22.0 0.1 copy.25
  22.1 3.0 %collective-permute-start = (bf16[2,64,256]{2,1,0:T(8,128)(2,1)S(1)}, bf16[2,64,256]{2,1,0:T(8,128)(2,1)S(1)}, u32[]{:S(2)}, u32[]{:S(2)}) collective-permute-start(bf16[2,64,256]{2,1,0:T(8,128)(2,1)S(1)} %bitcast.25), channel_id=1, source_target_pairs={{0,8},{1,9},{2,10},{3,11},{4,12},{5,13},{6,14},{7,15},{8,0},{9,1},... | collective-permute-start | bytes 196616 | tf_op jit(solution)/shard_map/ppermute | solution.py:271
  25.1 3.6 %all-to-all-start.1 = ((bf16[16,16,1024]{2,1,0:T(8,128)(2,1)}), bf16[16,16,1024]{2,1,0:T(8,128)(2,1)S(1)}, u32[]{:S(2)}, u32[]{:S(2)}) async-start(bf16[16,16,1024]{2,1,0:T(8,128)(2,1)} %bitcast.17), calls=%async_computation.1 | async-start | bytes 1048576 | tf_op jit(solution)/shard_map/all_to_all | solution.py:312
  28.7 0.0 collective-permute-done
  28.7 2.2 collective-permute-start.3
  30.9 0.0 collective-permute-start.2
  30.9 2.6 collective-permute-start.1
  33.5 2.9 %collective-permute-done.3.refs_3_ = bf16[4,64,256]{2,1,0:T(8,128)(2,1)S(1)} collective-permute-done((bf16[4,64,256]{2,1,0:T(8,128)(2,1)S(1)}, bf16[4,64,256]{2,1,0:T(8,128)(2,1)S(1)}, u32[]{:S(2)}, u32[]{:S(2)}) %collective-permute-start.3) | collective-permute-done | bytes 131104 | tf_op jit(solution)/shard_map/ppermute | solution.py:271
  36.4 1.7 collective-permute-done.2.refs_2_
  38.1 0.1 collective-permute-done.1.refs_1_
  38.2 216.5 %transforms.1.weights_ref = bf16[4,256,256]{2,1,0:T(8,128)(2,1)S(1)} custom-call(bf16[4,64,256]{2,1,0:T(8,128)(2,1)S(1)} %pad_maximum_fusion.refs_0_, bf16[4,64,256]{2,1,0:T(8,128)(2,1)S(1)} %collective-permute-done.1.refs_1_, bf16[4,64,256]{2,1,0:T(8,128)(2,1)S(1)} %collective-permute-done.2.refs_2_, ...), custom_call_target="tpu_custom_call" | custom-call | flops 8000000000 | bytes 1024 | tf_op jit(solution)/shard_map/transforms/pallas_call | solution.py:174
  254.7 0.0 all-to-all-done.1
  254.7 1.5 apply.1
  256.2 24.4 %all_to_all.15 = bf16[16,16,1024]{2,1,0:T(8,128)(2,1)S(1)} all-to-all(bf16[16,16,1024]{2,1,0:T(8,128)(2,1)S(1)} %bitcast.20), channel_id=1, replica_groups=mesh['mem'=16,'col'=16] {'mem'}, dimensions={0} | all-to-all | bytes 1048576 | tf_op jit(solution)/shard_map/all_to_all | solution.py:318
  280.6 0.8 copy.27
  (2 shorter events, 0.0 us)
Async XLA Ops:
  0.0 13.2 %copy-start.1 = (bf16[16,16384]{1,0:T(8,128)(2,1)S(1)}, bf16[16,16384]{1,0:T(8,128)(2,1)}, u32[]{:S(2)}) copy-start(bf16[16,16384]{1,0:T(8,128)(2,1)} %refs_1_.1) | copy-start | bytes 1572868
  2.3 9.9 %copy-start.2 = (s32[4,256]{1,0:T(4,128)S(1)}, s32[4,256]{1,0:T(4,128)}, u32[]{:S(2)}) copy-start(s32[4,256]{1,0:T(4,128)} %refs_2_.1) | copy-start | bytes 12292
  2.4 19.7 %all-to-all-start = ((bf16[32,16,128]{2,1,0:T(8,128)(2,1)}), bf16[32,16,128]{2,1,0:T(8,128)(2,1)S(1)}, u32[]{:S(2)}, u32[]{:S(2)}) async-start(bf16[32,16,128]{2,1,0:T(8,128)(2,1)} %select.17), calls=%async_computation | async-start | bytes 262144 | tf_op jit(solution)/shard_map/all_to_all | solution.py:300
  12.4 0.7 copy-start
  22.1 6.6 %collective-permute-start = (bf16[2,64,256]{2,1,0:T(8,128)(2,1)S(1)}, bf16[2,64,256]{2,1,0:T(8,128)(2,1)S(1)}, u32[]{:S(2)}, u32[]{:S(2)}) collective-permute-start(bf16[2,64,256]{2,1,0:T(8,128)(2,1)S(1)} %bitcast.25), channel_id=1, source_target_pairs={{0,8},{1,9},{2,10},{3,11},{4,12},{5,13},{6,14},{7,15},{8,0},{9,1},... | collective-permute-start | bytes 196616 | tf_op jit(solution)/shard_map/ppermute | solution.py:271
  25.1 229.6 %all-to-all-start.1 = ((bf16[16,16,1024]{2,1,0:T(8,128)(2,1)}), bf16[16,16,1024]{2,1,0:T(8,128)(2,1)S(1)}, u32[]{:S(2)}, u32[]{:S(2)}) async-start(bf16[16,16,1024]{2,1,0:T(8,128)(2,1)} %bitcast.17), calls=%async_computation.1 | async-start | bytes 1048576 | tf_op jit(solution)/shard_map/all_to_all | solution.py:312
  28.7 7.7 %collective-permute-start.3 = (bf16[4,64,256]{2,1,0:T(8,128)(2,1)S(1)}, bf16[4,64,256]{2,1,0:T(8,128)(2,1)S(1)}, u32[]{:S(2)}, u32[]{:S(2)}) collective-permute-start(bf16[4,64,256]{2,1,0:T(8,128)(2,1)S(1)} %pad_maximum_fusion.refs_0_), channel_id=1, source_target_pairs={{0,4},{1,5},{2,6},{3,7},{4,0},{5,1},{6,2},{7,3},{8,12},{9,13},{10,... | collective-permute-start | bytes 393224 | tf_op jit(solution)/shard_map/ppermute | solution.py:271
  30.9 7.2 %collective-permute-start.2 = (bf16[4,64,256]{2,1,0:T(8,128)(2,1)S(1)}, bf16[4,64,256]{2,1,0:T(8,128)(2,1)S(1)}, u32[]{:S(2)}, u32[]{:S(2)}) collective-permute-start(bf16[4,64,256]{2,1,0:T(8,128)(2,1)S(1)} %pad_maximum_fusion.refs_0_), channel_id=1, source_target_pairs={{0,6},{1,7},{2,4},{3,5},{4,2},{5,3},{6,0},{7,1},{8,14},{9,15},{10,... | collective-permute-start | bytes 393224 | tf_op jit(solution)/shard_map/ppermute | solution.py:271
  30.9 7.3 %collective-permute-start.1 = (bf16[4,64,256]{2,1,0:T(8,128)(2,1)S(1)}, bf16[4,64,256]{2,1,0:T(8,128)(2,1)S(1)}, u32[]{:S(2)}, u32[]{:S(2)}) collective-permute-start(bf16[4,64,256]{2,1,0:T(8,128)(2,1)S(1)} %pad_maximum_fusion.refs_0_), channel_id=1, source_target_pairs={{0,2},{1,3},{2,0},{3,1},{4,6},{5,7},{6,4},{7,5},{8,10},{9,11},{10,... | collective-permute-start | bytes 393224 | tf_op jit(solution)/shard_map/ppermute | solution.py:271

commit v6 on v5

--- a/solution.py
+++ b/solution.py
@@ -196,7 +196,7 @@
 def apply_kernel(weights_ref, block_ref, out_ref):
     batches = weights_ref.shape[0]
     columns = out_ref.shape[1]
-    chunk = min(columns, 512)
+    chunk = min(columns, 1024)
     for start in range(0, columns, chunk):
         piece = slice(start, start + chunk)
         part = block_ref[:, piece]

time: 282 us -> 281 us (level)
  no operation moved by 1% of the time
where the time goes in v6:
time: 281 us
  Pallas kernels  220 us (78%)
  blocking collectives  24.4 us (9%)
  starting transfers between devices  21.2 us (8%)
  waiting for transfers between devices  12.2 us (4%)
    pallas_call x1, Pallas kernels, transforms(): pl.pallas_call(lambda *refs: transform_kernel(*refs, inverse_count=1.0 /...  216 us
    all_to_all x1, blocking collectives, on_device(): lax.all_to_all(ensemble.reshape(mem_count, members_here, block_cols), 'me...  24.4 us
    all_to_all x1, starting transfers between devices, on_device(): lax.all_to_all(sent, ('mem', 'col'), split_axis=0, concat_axis=0, tiled=T...  9.88 us
    ppermute x4, starting transfers between devices, swapped(): return lax.ppermute(value, 'col', [(i, i ^ bits) for i in range(count)])  7.77 us
    all_to_all x1, waiting for transfers between devices, on_device(): lax.all_to_all(sent, ('mem', 'col'), split_axis=0, concat_axis=0, tiled=T...  7.5 us
  transfers between devices with their start and end apart: 6, of which 4 were waited for; matrix products, arithmetic and copies ran while one was open for 1% of the time, Pallas kernels for 77%

profile of v6, /device:TPU:2, one launch (start us, length us, event | category | flops | bytes accessed | tf_op | source)
XLA Modules:
  0.0 280.9 jit_solution(15206824626930638732)
XLA Ops:
  0.0 0.0 copy-start.1
  0.0 2.3 select.17
  2.3 0.0 copy-start.2
  2.4 9.9 %all-to-all-start = ((bf16[32,16,128]{2,1,0:T(8,128)(2,1)}), bf16[32,16,128]{2,1,0:T(8,128)(2,1)S(1)}, u32[]{:S(2)}, u32[]{:S(2)}) async-start(bf16[32,16,128]{2,1,0:T(8,128)(2,1)} %select.17), calls=%async_computation | async-start | bytes 262144 | tf_op jit(solution)/shard_map/all_to_all | solution.py:300
  12.2 0.0 copy-done.2
  12.3 0.1 copy.15
  12.4 0.0 copy-start
  12.4 0.2 copy.20
  12.6 0.5 copy-done
  13.1 0.1 copy.22
  13.2 0.0 copy-done.1
  13.3 0.8 copy.29
  14.1 0.4 fusion.6.refs_4_
  14.5 7.5 %all-to-all-done = bf16[32,16,128]{2,1,0:T(8,128)(2,1)S(1)} async-done(((bf16[32,16,128]{2,1,0:T(8,128)(2,1)}), bf16[32,16,128]{2,1,0:T(8,128)(2,1)S(1)}, u32[]{:S(2)}, u32[]{:S(2)}) %all-to-all-start) | async-done | bytes 131104 | tf_op jit(solution)/shard_map/all_to_all | solution.py:300
  22.0 0.1 copy.25
  22.1 3.0 %collective-permute-start = (bf16[2,64,256]{2,1,0:T(8,128)(2,1)S(1)}, bf16[2,64,256]{2,1,0:T(8,128)(2,1)S(1)}, u32[]{:S(2)}, u32[]{:S(2)}) collective-permute-start(bf16[2,64,256]{2,1,0:T(8,128)(2,1)S(1)} %bitcast.25), channel_id=1, source_target_pairs={{0,8},{1,9},{2,10},{3,11},{4,12},{5,13},{6,14},{7,15},{8,0},{9,1},... | collective-permute-start | bytes 196616 | tf_op jit(solution)/shard_map/ppermute | solution.py:271
  25.1 3.6 %all-to-all-start.1 = ((bf16[16,16,1024]{2,1,0:T(8,128)(2,1)}), bf16[16,16,1024]{2,1,0:T(8,128)(2,1)S(1)}, u32[]{:S(2)}, u32[]{:S(2)}) async-start(bf16[16,16,1024]{2,1,0:T(8,128)(2,1)} %bitcast.17), calls=%async_computation.1 | async-start | bytes 1048576 | tf_op jit(solution)/shard_map/all_to_all | solution.py:312
  28.7 0.0 collective-permute-done
  28.7 2.2 collective-permute-start.3
  30.9 0.0 collective-permute-start.2
  30.9 2.6 collective-permute-start.1
  33.5 2.9 %collective-permute-done.3.refs_3_ = bf16[4,64,256]{2,1,0:T(8,128)(2,1)S(1)} collective-permute-done((bf16[4,64,256]{2,1,0:T(8,128)(2,1)S(1)}, bf16[4,64,256]{2,1,0:T(8,128)(2,1)S(1)}, u32[]{:S(2)}, u32[]{:S(2)}) %collective-permute-start.3) | collective-permute-done | bytes 131104 | tf_op jit(solution)/shard_map/ppermute | solution.py:271
  36.4 1.7 collective-permute-done.2.refs_2_
  38.1 0.1 collective-permute-done.1.refs_1_
  38.2 216.5 %transforms.1.weights_ref = bf16[4,256,256]{2,1,0:T(8,128)(2,1)S(1)} custom-call(bf16[4,64,256]{2,1,0:T(8,128)(2,1)S(1)} %pad_maximum_fusion.refs_0_, bf16[4,64,256]{2,1,0:T(8,128)(2,1)S(1)} %collective-permute-done.1.refs_1_, bf16[4,64,256]{2,1,0:T(8,128)(2,1)S(1)} %collective-permute-done.2.refs_2_, ...), custom_call_target="tpu_custom_call" | custom-call | flops 8000000000 | bytes 1024 | tf_op jit(solution)/shard_map/transforms/pallas_call | solution.py:174
  254.7 0.0 all-to-all-done.1
  254.7 0.9 apply.1
  255.6 24.4 %all_to_all.15 = bf16[16,16,1024]{2,1,0:T(8,128)(2,1)S(1)} all-to-all(bf16[16,16,1024]{2,1,0:T(8,128)(2,1)S(1)} %bitcast.20), channel_id=1, replica_groups=mesh['mem'=16,'col'=16] {'mem'}, dimensions={0} | all-to-all | bytes 1048576 | tf_op jit(solution)/shard_map/all_to_all | solution.py:318
  280.1 0.8 copy.27
  (2 shorter events, 0.0 us)
Async XLA Ops:
  0.0 13.2 %copy-start.1 = (bf16[16,16384]{1,0:T(8,128)(2,1)S(1)}, bf16[16,16384]{1,0:T(8,128)(2,1)}, u32[]{:S(2)}) copy-start(bf16[16,16384]{1,0:T(8,128)(2,1)} %refs_1_.1) | copy-start | bytes 1572868
  2.3 9.9 %copy-start.2 = (s32[4,256]{1,0:T(4,128)S(1)}, s32[4,256]{1,0:T(4,128)}, u32[]{:S(2)}) copy-start(s32[4,256]{1,0:T(4,128)} %refs_2_.1) | copy-start | bytes 12292
  2.4 19.7 %all-to-all-start = ((bf16[32,16,128]{2,1,0:T(8,128)(2,1)}), bf16[32,16,128]{2,1,0:T(8,128)(2,1)S(1)}, u32[]{:S(2)}, u32[]{:S(2)}) async-start(bf16[32,16,128]{2,1,0:T(8,128)(2,1)} %select.17), calls=%async_computation | async-start | bytes 262144 | tf_op jit(solution)/shard_map/all_to_all | solution.py:300
  12.4 0.7 copy-start
  22.1 6.6 %collective-permute-start = (bf16[2,64,256]{2,1,0:T(8,128)(2,1)S(1)}, bf16[2,64,256]{2,1,0:T(8,128)(2,1)S(1)}, u32[]{:S(2)}, u32[]{:S(2)}) collective-permute-start(bf16[2,64,256]{2,1,0:T(8,128)(2,1)S(1)} %bitcast.25), channel_id=1, source_target_pairs={{0,8},{1,9},{2,10},{3,11},{4,12},{5,13},{6,14},{7,15},{8,0},{9,1},... | collective-permute-start | bytes 196616 | tf_op jit(solution)/shard_map/ppermute | solution.py:271
  25.1 229.6 %all-to-all-start.1 = ((bf16[16,16,1024]{2,1,0:T(8,128)(2,1)}), bf16[16,16,1024]{2,1,0:T(8,128)(2,1)S(1)}, u32[]{:S(2)}, u32[]{:S(2)}) async-start(bf16[16,16,1024]{2,1,0:T(8,128)(2,1)} %bitcast.17), calls=%async_computation.1 | async-start | bytes 1048576 | tf_op jit(solution)/shard_map/all_to_all | solution.py:312
  28.7 7.7 %collective-permute-start.3 = (bf16[4,64,256]{2,1,0:T(8,128)(2,1)S(1)}, bf16[4,64,256]{2,1,0:T(8,128)(2,1)S(1)}, u32[]{:S(2)}, u32[]{:S(2)}) collective-permute-start(bf16[4,64,256]{2,1,0:T(8,128)(2,1)S(1)} %pad_maximum_fusion.refs_0_), channel_id=1, source_target_pairs={{0,4},{1,5},{2,6},{3,7},{4,0},{5,1},{6,2},{7,3},{8,12},{9,13},{10,... | collective-permute-start | bytes 393224 | tf_op jit(solution)/shard_map/ppermute | solution.py:271
  30.9 7.2 %collective-permute-start.2 = (bf16[4,64,256]{2,1,0:T(8,128)(2,1)S(1)}, bf16[4,64,256]{2,1,0:T(8,128)(2,1)S(1)}, u32[]{:S(2)}, u32[]{:S(2)}) collective-permute-start(bf16[4,64,256]{2,1,0:T(8,128)(2,1)S(1)} %pad_maximum_fusion.refs_0_), channel_id=1, source_target_pairs={{0,6},{1,7},{2,4},{3,5},{4,2},{5,3},{6,0},{7,1},{8,14},{9,15},{10,... | collective-permute-start | bytes 393224 | tf_op jit(solution)/shard_map/ppermute | solution.py:271
  30.9 7.3 %collective-permute-start.1 = (bf16[4,64,256]{2,1,0:T(8,128)(2,1)S(1)}, bf16[4,64,256]{2,1,0:T(8,128)(2,1)S(1)}, u32[]{:S(2)}, u32[]{:S(2)}) collective-permute-start(bf16[4,64,256]{2,1,0:T(8,128)(2,1)S(1)} %pad_maximum_fusion.refs_0_), channel_id=1, source_target_pairs={{0,2},{1,3},{2,0},{3,1},{4,6},{5,7},{6,4},{7,5},{8,10},{9,11},{10,... | collective-permute-start | bytes 393224 | tf_op jit(solution)/shard_map/ppermute | solution.py:271

commit v7 on v6

--- a/solution.py
+++ b/solution.py
@@ -125,7 +125,7 @@
     (*part_refs, place_ref, var_ref, var_col_ref, weights_ref,
      obs_ref, obs_t_ref, lower_ref, upper_ref, cov_ref, inv_ref, shift_ref) = refs
     batches, observations = var_ref.shape
-    pieces, rows_held, members = part_refs[0].shape
+    _, rows_held, members = part_refs[0].shape
     per_batch = rows_held // batches
     rows, cols = iotas(observations)
     eye = jnp.where(rows == cols, 1.0, 0.0).astype(BF16)
@@ -134,7 +134,9 @@
         for batch in range(batches):
             order = jnp.where(cols == place_ref[:, batch : batch + 1], 1.0, 0.0)
             held = slice(batch * per_batch, (batch + 1) * per_batch)
-            parts = [ref[:, held, :].reshape(pieces * per_batch, members) for ref in part_refs]
+            parts = [
+                ref[:, held, :].reshape(ref.shape[0] * per_batch, members) for ref in part_refs
+            ]
             obs_t = mul(order, jnp.concatenate(parts)).astype(BF16)
             obs_t_ref[batch] = obs_t
             obs_ref[batch] = mul_t(eye, obs_t).astype(BF16)
@@ -272,8 +274,9 @@
 
 
 def gather_col(own, count):
+    across = swapped(own, 4, count)
     pair = jnp.concatenate([own, swapped(own, 8, count)])
-    return [pair] + [swapped(pair, bits, count) for bits in (2, 6, 4)]
+    return [pair, swapped(pair, 2, count), swapped(pair, 6, count), across, swapped(across, 8, count)]
 
 
 PIECES = [q ^ p for q in (0, 2, 6, 4) for p in (0, 8)]

time: 281 us -> 284 us (1.011); the launches traced: 281 us -> 281 us
    ppermute x4 -> x5, waiting for transfers between devices: 4.68 us -> 5.74 us  [swapped(): return lax.ppermute(value, 'col', [(i, i ^ bits) for i in range(count)])]
    ppermute x4 -> x5, starting transfers between devices: 7.77 us -> 8.53 us  [swapped(): return lax.ppermute(value, 'col', [(i, i ^ bits) for i in range(count)])]
  transfers between devices with their start and end apart: 6 -> 7, of which waited for: 4 -> 2; matrix products, arithmetic and copies ran while one was open for 1% -> 1% of each run, Pallas kernels for 77% -> 77%
where the time goes in v7:
time: 284 us; the launch traced here: 281 us
  Pallas kernels  220 us (77%)
  blocking collectives  22.6 us (8%)
  starting transfers between devices  22 us (8%)
  waiting for transfers between devices  13.3 us (5%)
    pallas_call x1, Pallas kernels, transforms(): pl.pallas_call(lambda *refs: transform_kernel(*refs, inverse_count=1.0 /...  216 us
    all_to_all x1, blocking collectives, on_device(): lax.all_to_all(ensemble.reshape(mem_count, members_here, block_cols), 'me...  22.6 us
    all_to_all x1, starting transfers between devices, on_device(): lax.all_to_all(sent, ('mem', 'col'), split_axis=0, concat_axis=0, tiled=T...  9.88 us
    ppermute x5, starting transfers between devices, swapped(): return lax.ppermute(value, 'col', [(i, i ^ bits) for i in range(count)])  8.53 us
    all_to_all x1, waiting for transfers between devices, on_device(): lax.all_to_all(sent, ('mem', 'col'), split_axis=0, concat_axis=0, tiled=T...  7.5 us
    ppermute x5, waiting for transfers between devices, swapped(): return lax.ppermute(value, 'col', [(i, i ^ bits) for i in range(count)])  5.74 us
  transfers between devices with their start and end apart: 7, of which 2 were waited for; matrix products, arithmetic and copies ran while one was open for 1% of the time, Pallas kernels for 77%

profile of v7, /device:TPU:2, one launch (start us, length us, event | category | flops | bytes accessed | tf_op | source)
XLA Modules:
  0.0 280.9 jit_solution(9056075994864956197)
XLA Ops:
  0.0 0.0 copy-start.1
  0.0 2.3 select.17
  2.3 0.0 copy-start.2
  2.3 9.9 %all-to-all-start = ((bf16[32,16,128]{2,1,0:T(8,128)(2,1)}), bf16[32,16,128]{2,1,0:T(8,128)(2,1)S(1)}, u32[]{:S(2)}, u32[]{:S(2)}) async-start(bf16[32,16,128]{2,1,0:T(8,128)(2,1)} %select.17), calls=%async_computation | async-start | bytes 262144 | tf_op jit(solution)/shard_map/all_to_all | solution.py:303
  12.2 0.0 copy-done.2
  12.3 0.1 copy.15
  12.4 0.0 copy-start
  12.4 0.2 copy.20
  12.6 0.5 copy-done
  13.1 0.1 copy.22
  13.2 0.0 copy-done.1
  13.2 0.8 copy.29
  14.1 0.4 fusion.6.refs_5_
  14.5 7.5 %all-to-all-done = bf16[32,16,128]{2,1,0:T(8,128)(2,1)S(1)} async-done(((bf16[32,16,128]{2,1,0:T(8,128)(2,1)}), bf16[32,16,128]{2,1,0:T(8,128)(2,1)S(1)}, u32[]{:S(2)}, u32[]{:S(2)}) %all-to-all-start) | async-done | bytes 131104 | tf_op jit(solution)/shard_map/all_to_all | solution.py:303
  22.0 0.1 copy.25
  22.1 3.0 %collective-permute-start = (bf16[2,64,256]{2,1,0:T(8,128)(2,1)S(1)}, bf16[2,64,256]{2,1,0:T(8,128)(2,1)S(1)}, u32[]{:S(2)}, u32[]{:S(2)}) collective-permute-start(bf16[2,64,256]{2,1,0:T(8,128)(2,1)S(1)} %bitcast.25), channel_id=1, source_target_pairs={{0,8},{1,9},{2,10},{3,11},{4,12},{5,13},{6,14},{7,15},{8,0},{9,1},... | collective-permute-start | bytes 196616 | tf_op jit(solution)/shard_map/ppermute | solution.py:273
  25.1 2.1 collective-permute-start.3
  27.2 3.6 %all-to-all-start.1 = ((bf16[16,16,1024]{2,1,0:T(8,128)(2,1)}), bf16[16,16,1024]{2,1,0:T(8,128)(2,1)S(1)}, u32[]{:S(2)}, u32[]{:S(2)}) async-start(bf16[16,16,1024]{2,1,0:T(8,128)(2,1)} %bitcast.17), calls=%async_computation.1 | async-start | bytes 1048576 | tf_op jit(solution)/shard_map/all_to_all | solution.py:315
  30.8 0.0 collective-permute-done
  30.8 0.1 collective-permute-start.2
  30.9 2.6 collective-permute-start.1
  33.5 0.0 collective-permute-done.3.refs_3_
  33.5 0.8 collective-permute-start.4
  34.3 5.7 %collective-permute-done.4.refs_4_ = bf16[2,64,256]{2,1,0:T(8,128)(2,1)S(1)} collective-permute-done((bf16[2,64,256]{2,1,0:T(8,128)(2,1)S(1)}, bf16[2,64,256]{2,1,0:T(8,128)(2,1)S(1)}, u32[]{:S(2)}, u32[]{:S(2)}) %collective-permute-start.4) | collective-permute-done | bytes 65568 | tf_op jit(solution)/shard_map/ppermute | solution.py:273
  40.0 0.0 collective-permute-done.2.refs_2_
  40.0 0.0 collective-permute-done.1.refs_1_
  40.0 216.5 %transforms.1.weights_ref = bf16[4,256,256]{2,1,0:T(8,128)(2,1)S(1)} custom-call(bf16[4,64,256]{2,1,0:T(8,128)(2,1)S(1)} %pad_maximum_fusion.refs_0_, bf16[4,64,256]{2,1,0:T(8,128)(2,1)S(1)} %collective-permute-done.1.refs_1_, bf16[4,64,256]{2,1,0:T(8,128)(2,1)S(1)} %collective-permute-done.2.refs_2_, ...), custom_call_target="tpu_custom_call" | custom-call | flops 8000000000 | bytes 1024 | tf_op jit(solution)/shard_map/transforms/pallas_call | solution.py:176
  256.5 0.0 all-to-all-done.1
  256.5 0.9 apply.1
  257.4 22.6 %all_to_all.15 = bf16[16,16,1024]{2,1,0:T(8,128)(2,1)S(1)} all-to-all(bf16[16,16,1024]{2,1,0:T(8,128)(2,1)S(1)} %bitcast.20), channel_id=1, replica_groups=mesh['mem'=16,'col'=16] {'mem'}, dimensions={0} | all-to-all | bytes 1048576 | tf_op jit(solution)/shard_map/all_to_all | solution.py:321
  280.0 0.8 copy.27
  (2 shorter events, 0.0 us)
Async XLA Ops:
  0.0 13.2 %copy-start.1 = (bf16[16,16384]{1,0:T(8,128)(2,1)S(1)}, bf16[16,16384]{1,0:T(8,128)(2,1)}, u32[]{:S(2)}) copy-start(bf16[16,16384]{1,0:T(8,128)(2,1)} %refs_1_.1) | copy-start | bytes 1572868
  2.3 9.9 %copy-start.2 = (s32[4,256]{1,0:T(4,128)S(1)}, s32[4,256]{1,0:T(4,128)}, u32[]{:S(2)}) copy-start(s32[4,256]{1,0:T(4,128)} %refs_2_.1) | copy-start | bytes 12292
  2.3 19.7 %all-to-all-start = ((bf16[32,16,128]{2,1,0:T(8,128)(2,1)}), bf16[32,16,128]{2,1,0:T(8,128)(2,1)S(1)}, u32[]{:S(2)}, u32[]{:S(2)}) async-start(bf16[32,16,128]{2,1,0:T(8,128)(2,1)} %select.17), calls=%async_computation | async-start | bytes 262144 | tf_op jit(solution)/shard_map/all_to_all | solution.py:303
  12.4 0.7 copy-start
  22.1 8.7 %collective-permute-start = (bf16[2,64,256]{2,1,0:T(8,128)(2,1)S(1)}, bf16[2,64,256]{2,1,0:T(8,128)(2,1)S(1)}, u32[]{:S(2)}, u32[]{:S(2)}) collective-permute-start(bf16[2,64,256]{2,1,0:T(8,128)(2,1)S(1)} %bitcast.25), channel_id=1, source_target_pairs={{0,8},{1,9},{2,10},{3,11},{4,12},{5,13},{6,14},{7,15},{8,0},{9,1},... | collective-permute-start | bytes 196616 | tf_op jit(solution)/shard_map/ppermute | solution.py:273
  25.1 8.4 %collective-permute-start.3 = (bf16[2,64,256]{2,1,0:T(8,128)(2,1)S(1)}, bf16[2,64,256]{2,1,0:T(8,128)(2,1)S(1)}, u32[]{:S(2)}, u32[]{:S(2)}) collective-permute-start(bf16[2,64,256]{2,1,0:T(8,128)(2,1)S(1)} %bitcast.26), channel_id=1, source_target_pairs={{0,4},{1,5},{2,6},{3,7},{4,0},{5,1},{6,2},{7,3},{8,12},{9,13},{10,... | collective-permute-start | bytes 196616 | tf_op jit(solution)/shard_map/ppermute | solution.py:273
  27.2 229.3 %all-to-all-start.1 = ((bf16[16,16,1024]{2,1,0:T(8,128)(2,1)}), bf16[16,16,1024]{2,1,0:T(8,128)(2,1)S(1)}, u32[]{:S(2)}, u32[]{:S(2)}) async-start(bf16[16,16,1024]{2,1,0:T(8,128)(2,1)} %bitcast.17), calls=%async_computation.1 | async-start | bytes 1048576 | tf_op jit(solution)/shard_map/all_to_all | solution.py:315
  30.8 9.2 %collective-permute-start.2 = (bf16[4,64,256]{2,1,0:T(8,128)(2,1)S(1)}, bf16[4,64,256]{2,1,0:T(8,128)(2,1)S(1)}, u32[]{:S(2)}, u32[]{:S(2)}) collective-permute-start(bf16[4,64,256]{2,1,0:T(8,128)(2,1)S(1)} %pad_maximum_fusion.refs_0_), channel_id=1, source_target_pairs={{0,6},{1,7},{2,4},{3,5},{4,2},{5,3},{6,0},{7,1},{8,14},{9,15},{10,... | collective-permute-start | bytes 393224 | tf_op jit(solution)/shard_map/ppermute | solution.py:273
  30.9 9.1 %collective-permute-start.1 = (bf16[4,64,256]{2,1,0:T(8,128)(2,1)S(1)}, bf16[4,64,256]{2,1,0:T(8,128)(2,1)S(1)}, u32[]{:S(2)}, u32[]{:S(2)}) collective-permute-start(bf16[4,64,256]{2,1,0:T(8,128)(2,1)S(1)} %pad_maximum_fusion.refs_0_), channel_id=1, source_target_pairs={{0,2},{1,3},{2,0},{3,1},{4,6},{5,7},{6,4},{7,5},{8,10},{9,11},{10,... | collective-permute-start | bytes 393224 | tf_op jit(solution)/shard_map/ppermute | solution.py:273
  33.5 6.5 %collective-permute-start.4 = (bf16[2,64,256]{2,1,0:T(8,128)(2,1)S(1)}, bf16[2,64,256]{2,1,0:T(8,128)(2,1)S(1)}, u32[]{:S(2)}, u32[]{:S(2)}) collective-permute-start(bf16[2,64,256]{2,1,0:T(8,128)(2,1)S(1)} %collective-permute-done.3.refs_3_), channel_id=1, source_target_pairs={{0,8},{1,9},{2,10},{3,11},{4,12},{5,13},{6,14},{7,15},{8,0},{9,1},... | collective-permute-start | bytes 196616 | tf_op jit(solution)/shard_map/ppermute | solution.py:273

commit v8 on v6

--- a/solution.py
+++ b/solution.py
@@ -10,7 +10,8 @@
 F32 = jnp.float32
 BF16 = jnp.bfloat16
 START = 0.86
-STRETCH = (1.07, 1.003)
+STRETCH = 1.07
+STEPS = 3
 RESIDUAL_MAX = 3e-2
 B_WEIGHT = 300.0
 PAD = 128
@@ -34,35 +35,34 @@
     return rows, cols
 
 
-def fast_transform(obs, obs_t, var_row, var_col, lower_ref, upper_ref, inverse_count):
-    n = obs.shape[1]
-    rows, cols = iotas(n)
+def fast_transform(obs, obs_t, var_row, var_col, eye_ref, lower_ref, upper_ref, inverse_count):
     wide = obs.astype(F32)
     wide_t = obs_t.astype(F32)
     dr = lax.rsqrt(jnp.sum(wide * wide, axis=0, keepdims=True) * inverse_count + var_row)
     dc = lax.rsqrt(jnp.sum(wide_t * wide_t, axis=1, keepdims=True) * inverse_count + var_col)
-    gram = mul_t(obs_t, obs_t)
-    error = jnp.where(rows == cols, START - 1.0, gram * (dc * (START * inverse_count)) * dr)
-    size = math.sqrt(START * math.prod(STRETCH))
+    rows, cols = iotas(obs.shape[1])
+    near = mul_t(obs_t, obs_t) * (dc * (-START * inverse_count)) * dr
+    near = jnp.where(rows == cols, 1.0 - START, near).astype(BF16)
+    size = math.sqrt(START * STRETCH)
     first_t = wide * (dr * (size * math.sqrt(inverse_count)))
     factor = None
-    for step in range(len(STRETCH) + 1):
-        near = error.astype(BF16)
+    for step in range(STEPS):
         f = near * lower_ref[...]
         if step == 0:
-            factor = jnp.where(rows == cols, size, 0.0) - size * f.astype(F32)
+            factor = (eye_ref[...] - f.astype(F32)) * size
         else:
             factor = factor - mul(f, factor)
         first_t = first_t - mul_t(first_t, f)
-        if step < len(STRETCH):
+        if step < STEPS - 1:
             w = mul(f, near)
-            y = near * upper_ref[...] - w.astype(BF16)
-            error = (error - near.astype(F32)) - (w + mul_t(y, f))
-            stretch = STRETCH[step]
-            error = error * stretch + jnp.where(rows == cols, stretch - 1.0, 0.0)
+            y = near * upper_ref[...] + w.astype(BF16)
+            error = mul_t(y, f) - w
+            if step == 0:
+                error = error * STRETCH - eye_ref[...] * (STRETCH - 1.0)
+            near = error.astype(BF16)
     left = jnp.sum(error * error, axis=0, keepdims=True)
     x = jnp.sqrt(var_row) * dr
-    diagonal = jnp.sum(jnp.where(rows == cols, factor, 0.0), axis=0, keepdims=True) * x
+    diagonal = jnp.sum(eye_ref[...] * factor, axis=0, keepdims=True) * x
     scale = 1.0 / (1.0 + diagonal)
     b = jnp.where(rows > cols, factor * (x * scale), 0.0).astype(BF16)
     b2 = mul(b, b).astype(BF16)
@@ -73,9 +73,8 @@
     left = left + B_WEIGHT * jnp.sum(b4 * b4, axis=0, keepdims=True)
     second_t = second_t.astype(BF16)
     first_t = first_t.astype(BF16)
-    one = jnp.where(rows == cols, 1.0, 0.0)
-    turned = (one - mul_t(second_t, first_t)).astype(BF16)
-    transform = (one - mul_t(first_t, second_t)).astype(BF16)
+    turned = (eye_ref[...] - mul_t(second_t, first_t)).astype(BF16)
+    transform = (eye_ref[...] - mul_t(first_t, second_t)).astype(BF16)
     return transform, turned, left
 
 
@@ -123,7 +122,7 @@
     *refs, inverse_count
 ):
     (*part_refs, place_ref, var_ref, var_col_ref, weights_ref,
-     obs_ref, obs_t_ref, lower_ref, upper_ref, cov_ref, inv_ref, shift_ref) = refs
+     obs_ref, obs_t_ref, eye_ref, lower_ref, upper_ref, cov_ref, inv_ref, shift_ref) = refs
     batches, observations = var_ref.shape
     pieces, rows_held, members = part_refs[0].shape
     per_batch = rows_held // batches
@@ -146,13 +145,14 @@
             obs_ref[later] = mul(weights, obs_ref[later]).astype(BF16)
 
     load()
-    lower_ref[...] = jnp.where(rows > cols, 1.0, jnp.where(rows == cols, 0.5, 0.0)).astype(BF16)
-    upper_ref[...] = jnp.where(rows < cols, 1.0, jnp.where(rows == cols, 0.5, 0.0)).astype(BF16)
+    eye_ref[...] = jnp.where(rows == cols, 1.0, 0.0)
+    lower_ref[...] = jnp.where(rows > cols, -1.0, jnp.where(rows == cols, -0.5, 0.0)).astype(BF16)
+    upper_ref[...] = jnp.where(rows < cols, -1.0, jnp.where(rows == cols, -0.5, 0.0)).astype(BF16)
     left = jnp.zeros((1, observations), F32)
     for batch in range(batches):
         weights, turned, part = fast_transform(
             obs_ref[batch], obs_t_ref[batch], var_ref[batch : batch + 1, :],
-            var_col_ref[:, batch : batch + 1], lower_ref, upper_ref, inverse_count,
+            var_col_ref[:, batch : batch + 1], eye_ref, lower_ref, upper_ref, inverse_count,
         )
         left = left + part
         advance(weights, turned, batch)
@@ -181,6 +181,7 @@
         scratch_shapes=[
             pltpu.VMEM((batches, members, observations), BF16),
             pltpu.VMEM((batches, observations, members), BF16),
+            pltpu.VMEM(square, F32),
             pltpu.VMEM(square, BF16),
             pltpu.VMEM(square, BF16),
             pltpu.VMEM(square, F32),

time: 281 us -> 282 us (level)
  no operation moved by 1% of the time
where the time goes in v8:
time: 282 us
  Pallas kernels  221 us (78%)
  blocking collectives  24.4 us (9%)
  starting transfers between devices  21.2 us (8%)
  waiting for transfers between devices  12.2 us (4%)
    pallas_call x1, Pallas kernels, transforms(): pl.pallas_call(lambda *refs: transform_kernel(*refs, inverse_count=1.0 /...  218 us
    all_to_all x1, blocking collectives, on_device(): lax.all_to_all(ensemble.reshape(mem_count, members_here, block_cols), 'me...  24.4 us
    all_to_all x1, starting transfers between devices, on_device(): lax.all_to_all(sent, ('mem', 'col'), split_axis=0, concat_axis=0, tiled=T...  9.88 us
    ppermute x4, starting transfers between devices, swapped(): return lax.ppermute(value, 'col', [(i, i ^ bits) for i in range(count)])  7.77 us
    all_to_all x1, waiting for transfers between devices, on_device(): lax.all_to_all(sent, ('mem', 'col'), split_axis=0, concat_axis=0, tiled=T...  7.5 us
  transfers between devices with their start and end apart: 6, of which 4 were waited for; matrix products, arithmetic and copies ran while one was open for 1% of the time, Pallas kernels for 77%

profile of v8, /device:TPU:2, one launch (start us, length us, event | category | flops | bytes accessed | tf_op | source)
XLA Modules:
  0.0 281.9 jit_solution(4818607106433997696)
XLA Ops:
  0.0 0.0 copy-start.1
  0.0 2.3 select.17
  2.3 0.0 copy-start.2
  2.4 9.9 %all-to-all-start = ((bf16[32,16,128]{2,1,0:T(8,128)(2,1)}), bf16[32,16,128]{2,1,0:T(8,128)(2,1)S(1)}, u32[]{:S(2)}, u32[]{:S(2)}) async-start(bf16[32,16,128]{2,1,0:T(8,128)(2,1)} %select.17), calls=%async_computation | async-start | bytes 262144 | tf_op jit(solution)/shard_map/all_to_all | solution.py:301
  12.2 0.0 copy-done.2
  12.3 0.1 copy.15
  12.4 0.0 copy-start
  12.4 0.2 copy.20
  12.6 0.5 copy-done
  13.1 0.1 copy.22
  13.2 0.0 copy-done.1
  13.3 0.8 copy.29
  14.1 0.4 fusion.6.refs_4_
  14.5 7.5 %all-to-all-done = bf16[32,16,128]{2,1,0:T(8,128)(2,1)S(1)} async-done(((bf16[32,16,128]{2,1,0:T(8,128)(2,1)}), bf16[32,16,128]{2,1,0:T(8,128)(2,1)S(1)}, u32[]{:S(2)}, u32[]{:S(2)}) %all-to-all-start) | async-done | bytes 131104 | tf_op jit(solution)/shard_map/all_to_all | solution.py:301
  22.0 0.1 copy.25
  22.1 3.0 %collective-permute-start = (bf16[2,64,256]{2,1,0:T(8,128)(2,1)S(1)}, bf16[2,64,256]{2,1,0:T(8,128)(2,1)S(1)}, u32[]{:S(2)}, u32[]{:S(2)}) collective-permute-start(bf16[2,64,256]{2,1,0:T(8,128)(2,1)S(1)} %bitcast.25), channel_id=1, source_target_pairs={{0,8},{1,9},{2,10},{3,11},{4,12},{5,13},{6,14},{7,15},{8,0},{9,1},... | collective-permute-start | bytes 196616 | tf_op jit(solution)/shard_map/ppermute | solution.py:272
  25.1 3.6 %all-to-all-start.1 = ((bf16[16,16,1024]{2,1,0:T(8,128)(2,1)}), bf16[16,16,1024]{2,1,0:T(8,128)(2,1)S(1)}, u32[]{:S(2)}, u32[]{:S(2)}) async-start(bf16[16,16,1024]{2,1,0:T(8,128)(2,1)} %bitcast.17), calls=%async_computation.1 | async-start | bytes 1048576 | tf_op jit(solution)/shard_map/all_to_all | solution.py:313
  28.7 0.0 collective-permute-done
  28.7 2.2 collective-permute-start.3
  30.9 0.0 collective-permute-start.2
  30.9 2.6 collective-permute-start.1
  33.5 2.9 %collective-permute-done.3.refs_3_ = bf16[4,64,256]{2,1,0:T(8,128)(2,1)S(1)} collective-permute-done((bf16[4,64,256]{2,1,0:T(8,128)(2,1)S(1)}, bf16[4,64,256]{2,1,0:T(8,128)(2,1)S(1)}, u32[]{:S(2)}, u32[]{:S(2)}) %collective-permute-start.3) | collective-permute-done | bytes 131104 | tf_op jit(solution)/shard_map/ppermute | solution.py:272
  36.4 1.7 collective-permute-done.2.refs_2_
  38.1 0.1 collective-permute-done.1.refs_1_
  38.2 217.5 %transforms.1.weights_ref = bf16[4,256,256]{2,1,0:T(8,128)(2,1)S(1)} custom-call(bf16[4,64,256]{2,1,0:T(8,128)(2,1)S(1)} %pad_maximum_fusion.refs_0_, bf16[4,64,256]{2,1,0:T(8,128)(2,1)S(1)} %collective-permute-done.1.refs_1_, bf16[4,64,256]{2,1,0:T(8,128)(2,1)S(1)} %collective-permute-done.2.refs_2_, ...), custom_call_target="tpu_custom_call" | custom-call | flops 8000000000 | bytes 1024 | tf_op jit(solution)/shard_map/transforms/pallas_call | solution.py:174
  255.7 0.0 all-to-all-done.1
  255.7 0.9 apply.1
  256.7 24.4 %all_to_all.15 = bf16[16,16,1024]{2,1,0:T(8,128)(2,1)S(1)} all-to-all(bf16[16,16,1024]{2,1,0:T(8,128)(2,1)S(1)} %bitcast.20), channel_id=1, replica_groups=mesh['mem'=16,'col'=16] {'mem'}, dimensions={0} | all-to-all | bytes 1048576 | tf_op jit(solution)/shard_map/all_to_all | solution.py:319
  281.1 0.8 copy.27
  (2 shorter events, 0.0 us)
Async XLA Ops:
  0.0 13.2 %copy-start.1 = (bf16[16,16384]{1,0:T(8,128)(2,1)S(1)}, bf16[16,16384]{1,0:T(8,128)(2,1)}, u32[]{:S(2)}) copy-start(bf16[16,16384]{1,0:T(8,128)(2,1)} %refs_1_.1) | copy-start | bytes 1572868
  2.3 9.9 %copy-start.2 = (s32[4,256]{1,0:T(4,128)S(1)}, s32[4,256]{1,0:T(4,128)}, u32[]{:S(2)}) copy-start(s32[4,256]{1,0:T(4,128)} %refs_2_.1) | copy-start | bytes 12292
  2.4 19.7 %all-to-all-start = ((bf16[32,16,128]{2,1,0:T(8,128)(2,1)}), bf16[32,16,128]{2,1,0:T(8,128)(2,1)S(1)}, u32[]{:S(2)}, u32[]{:S(2)}) async-start(bf16[32,16,128]{2,1,0:T(8,128)(2,1)} %select.17), calls=%async_computation | async-start | bytes 262144 | tf_op jit(solution)/shard_map/all_to_all | solution.py:301
  12.4 0.7 copy-start
  22.1 6.6 %collective-permute-start = (bf16[2,64,256]{2,1,0:T(8,128)(2,1)S(1)}, bf16[2,64,256]{2,1,0:T(8,128)(2,1)S(1)}, u32[]{:S(2)}, u32[]{:S(2)}) collective-permute-start(bf16[2,64,256]{2,1,0:T(8,128)(2,1)S(1)} %bitcast.25), channel_id=1, source_target_pairs={{0,8},{1,9},{2,10},{3,11},{4,12},{5,13},{6,14},{7,15},{8,0},{9,1},... | collective-permute-start | bytes 196616 | tf_op jit(solution)/shard_map/ppermute | solution.py:272
  25.1 230.6 %all-to-all-start.1 = ((bf16[16,16,1024]{2,1,0:T(8,128)(2,1)}), bf16[16,16,1024]{2,1,0:T(8,128)(2,1)S(1)}, u32[]{:S(2)}, u32[]{:S(2)}) async-start(bf16[16,16,1024]{2,1,0:T(8,128)(2,1)} %bitcast.17), calls=%async_computation.1 | async-start | bytes 1048576 | tf_op jit(solution)/shard_map/all_to_all | solution.py:313
  28.7 7.7 %collective-permute-start.3 = (bf16[4,64,256]{2,1,0:T(8,128)(2,1)S(1)}, bf16[4,64,256]{2,1,0:T(8,128)(2,1)S(1)}, u32[]{:S(2)}, u32[]{:S(2)}) collective-permute-start(bf16[4,64,256]{2,1,0:T(8,128)(2,1)S(1)} %pad_maximum_fusion.refs_0_), channel_id=1, source_target_pairs={{0,4},{1,5},{2,6},{3,7},{4,0},{5,1},{6,2},{7,3},{8,12},{9,13},{10,... | collective-permute-start | bytes 393224 | tf_op jit(solution)/shard_map/ppermute | solution.py:272
  30.9 7.2 %collective-permute-start.2 = (bf16[4,64,256]{2,1,0:T(8,128)(2,1)S(1)}, bf16[4,64,256]{2,1,0:T(8,128)(2,1)S(1)}, u32[]{:S(2)}, u32[]{:S(2)}) collective-permute-start(bf16[4,64,256]{2,1,0:T(8,128)(2,1)S(1)} %pad_maximum_fusion.refs_0_), channel_id=1, source_target_pairs={{0,6},{1,7},{2,4},{3,5},{4,2},{5,3},{6,0},{7,1},{8,14},{9,15},{10,... | collective-permute-start | bytes 393224 | tf_op jit(solution)/shard_map/ppermute | solution.py:272
  30.9 7.3 %collective-permute-start.1 = (bf16[4,64,256]{2,1,0:T(8,128)(2,1)S(1)}, bf16[4,64,256]{2,1,0:T(8,128)(2,1)S(1)}, u32[]{:S(2)}, u32[]{:S(2)}) collective-permute-start(bf16[4,64,256]{2,1,0:T(8,128)(2,1)S(1)} %pad_maximum_fusion.refs_0_), channel_id=1, source_target_pairs={{0,2},{1,3},{2,0},{3,1},{4,6},{5,7},{6,4},{7,5},{8,10},{9,11},{10,... | collective-permute-start | bytes 393224 | tf_op jit(solution)/shard_map/ppermute | solution.py:272
